TPU v7x, 512 devices: a whole 4x4x16 slice. The times are simulated.
512 devices in a mesh: lon: 16 (over z), lat: 8 (over x_lo, y), ch: 4 (over x_hi, core).
Axes of the slice: x: 4 (x_hi: 2, x_lo: 2; x = x_hi * 2 + x_lo), y: 4, z: 16, core: 2. Of those that a mesh axis runs over, the one named last changes fastest.
Arguments:
- ocean_state: bfloat16 [300, 256, 2048], P('ch', 'lat', 'lon'), may hold values from -6 to 6
- land_mask: int32 [256, 2048], P('lat', 'lon'), may hold values 0 or 1
- out_grad: bfloat16 [300, 256, 2048], P('ch', 'lat', 'lon'), may hold values from -6 to 6
- swath_offset: int32 [8, 16, 512], P('lat', 'lon'), may hold values from 0 to 4095
- swath_value: float32 [8, 16, 512], P('lat', 'lon'), may hold values from -8 to 8
- depth_kernel: float32 [3, 3, 300], P(None, None, 'ch'), may hold values from -2.5 to 2.5
- expand_weight: bfloat16 [300, 600], P(None, 'ch'), may hold values from -0.375 to 0.375
- expand_bias: float32 [600], P('ch'), may hold values from -3 to 3
- project_weight: bfloat16 [600, 300], P('ch'), may hold values from -0.25 to 0.25
Outputs:
- state_grad: bfloat16 [300, 256, 2048], P('ch', 'lat', 'lon')
- expand_grad: float32 [300, 600], P(None, 'ch')
- project_grad: float32 [600, 300], P('ch')
- bias_grad: float32 [600], P('ch')
- kernel_grad: float32 [3, 3, 300], P(None, None, 'ch')
Inputs may be any that keep to these rules, and one draw needn't show every extreme that they name: `swath_offset`: position of a swath point in row-major order over the 32 x 128 cells of its device's block.
All inputs are finite; a program needn't handle non-finite values. No bound on the sum of `land_mask` on one device may be relied on, other than what follows from the above.
Results may differ from a plain program's by a relative error of at most 0.014.
Values may be sent and summed in bfloat16 or wider, within the bound.
A program may use at most 64 MiB of HBM per device.

v0:
```python
import math

import jax
import jax.numpy as jnp
from jax import lax
from jax.sharding import PartitionSpec as P

DILATION_STEP = 2


def with_halo(block, sides, width):
    for axis, dim in sides:
        count = lax.axis_size(axis)
        forward = [(i, i + 1) for i in range(count - 1)]
        forward.append((count - 1, 0))
        backward = [(target, source) for source, target in forward]
        low = lax.ppermute(
            lax.slice_in_dim(block, block.shape[dim] - width, None, axis=dim), axis, forward
        )
        high = lax.ppermute(lax.slice_in_dim(block, 0, width, axis=dim), axis, backward)
        block = jnp.concatenate([low, block, high], axis=dim)
    return block


def extend(ocean_field):
    count_of_rows = ocean_field.shape[1]
    column_count = ocean_field.shape[2]
    halo_padded = with_halo(ocean_field, (("lon", 2), ("lat", 1)), DILATION_STEP)
    uppermost_rows = ocean_field[:, count_of_rows - DILATION_STEP :, :]
    gathered = lax.all_gather(uppermost_rows, "lon", axis=2, tiled=True)
    seam_mirrored = gathered[:, ::-1, ::-1]
    seam_mirrored = jnp.concatenate(
        [seam_mirrored[:, :, -DILATION_STEP:], seam_mirrored, seam_mirrored[:, :, :DILATION_STEP]],
        axis=2,
    )
    northern_border = lax.dynamic_slice_in_dim(
        seam_mirrored, lax.axis_index("lon") * column_count, column_count + 2 * DILATION_STEP, 2
    )
    latitude_index = lax.axis_index("lat")
    southern_boundary = halo_padded[:, :DILATION_STEP, :]
    southern_border = jnp.where(
        latitude_index == 0, jnp.zeros_like(southern_boundary), southern_boundary
    )
    northern_border = jnp.where(
        latitude_index == lax.axis_size("lat") - 1,
        northern_border,
        halo_padded[:, count_of_rows + DILATION_STEP :, :],
    )
    return jnp.concatenate(
        [
            southern_border,
            halo_padded[:, DILATION_STEP : count_of_rows + DILATION_STEP, :],
            northern_border,
        ],
        axis=1,
    )


def on_device(
    ocean_state,
    land_mask,
    out_grad,
    swath_offset,
    swath_value,
    depth_kernel,
    expand_weight,
    expand_bias,
    project_weight,
):
    channels_per_shard = ocean_state.shape[0]
    count_of_rows = ocean_state.shape[1]
    column_count = ocean_state.shape[2]
    cells = count_of_rows * column_count
    scale = 1.0 / math.sqrt(
        count_of_rows * lax.axis_size("lat") * column_count * lax.axis_size("lon")
    )
    mask_float = land_mask.astype(jnp.float32)[None]
    masked = ocean_state * land_mask.astype(jnp.bfloat16)[None]
    state_pad = extend(masked)
    forward = jnp.zeros((channels_per_shard, count_of_rows, column_count), jnp.float32)
    for row_offset in range(3):
        for column_offset in range(3):
            kernel_window = state_pad[
                :,
                DILATION_STEP * row_offset : DILATION_STEP * row_offset + count_of_rows,
                DILATION_STEP * column_offset : DILATION_STEP * column_offset + column_count,
            ]
            forward = forward + depth_kernel[row_offset, column_offset][
                :, None, None
            ] * kernel_window.astype(jnp.float32)
    conv_out = forward.astype(jnp.bfloat16)
    swath = (
        jnp.zeros((cells,), jnp.float32).at[swath_offset.reshape(-1)].add(swath_value.reshape(-1))
    )
    first_group = jnp.where(lax.axis_index("ch") == 0, 1.0, 0.0).astype(jnp.float32)
    cotan = (
        out_grad.astype(jnp.float32)
        .at[0]
        .add(first_group * swath.reshape(count_of_rows, column_count))
    )
    cotan = (cotan * mask_float).astype(jnp.bfloat16)
    conv_all, cotan_all = (
        lax.all_gather(conv_out, "ch", axis=0, tiled=True),
        lax.all_gather(cotan, "ch", axis=0, tiled=True),
    )
    conv_flat = conv_all.reshape(conv_all.shape[0], cells)
    cotan_flat = cotan_all.reshape(cotan_all.shape[0], cells)
    hidden = (
        jnp.dot(expand_weight.T, conv_flat, preferred_element_type=jnp.float32)
        + expand_bias[:, None]
    )
    activ, gelu_back = jax.vjp(jax.nn.gelu, hidden)
    act_grad = jnp.dot(project_weight, cotan_flat, preferred_element_type=jnp.float32)
    pre_grad = gelu_back(act_grad)[0].astype(jnp.bfloat16)
    project_part = (
        jnp.dot(activ.astype(jnp.bfloat16), cotan_flat.T, preferred_element_type=jnp.float32)
        * scale
    )
    expand_part = jnp.dot(conv_flat, pre_grad.T, preferred_element_type=jnp.float32) * scale
    bias_part = jnp.sum(pre_grad.astype(jnp.float32), axis=1) * scale
    summed = lax.psum_scatter(
        jnp.dot(expand_weight, pre_grad, preferred_element_type=jnp.float32).astype(jnp.bfloat16),
        "ch",
        scatter_dimension=0,
        tiled=True,
    )
    conv_grad = summed.reshape(channels_per_shard, count_of_rows, column_count)
    grad_pad = extend(conv_grad)
    grad_float = conv_grad.astype(jnp.float32)
    kernel_rows = []
    swapped_axes = jnp.zeros((channels_per_shard, count_of_rows, column_count), jnp.float32)
    for row_offset in range(3):
        kernel_cols = []
        for column_offset in range(3):
            kernel_window = state_pad[
                :,
                DILATION_STEP * row_offset : DILATION_STEP * row_offset + count_of_rows,
                DILATION_STEP * column_offset : DILATION_STEP * column_offset + column_count,
            ]
            kernel_cols.append(jnp.sum(grad_float * kernel_window.astype(jnp.float32), axis=(1, 2)))
            reverse_row = DILATION_STEP * (2 - row_offset)
            reverse_column = DILATION_STEP * (2 - column_offset)
            back_window = grad_pad[
                :,
                reverse_row : reverse_row + count_of_rows,
                reverse_column : reverse_column + column_count,
            ]
            swapped_axes = swapped_axes + depth_kernel[row_offset, column_offset][
                :, None, None
            ] * back_window.astype(jnp.float32)
        kernel_rows.append(jnp.stack(kernel_cols, axis=0))
    kernel_part = jnp.stack(kernel_rows, axis=0) * scale
    fold_adjustment = jnp.zeros((channels_per_shard, DILATION_STEP, column_count), jnp.float32)
    for column_offset in range(3):
        reverse_column = DILATION_STEP * (2 - column_offset)
        rim_window = grad_pad[
            :,
            count_of_rows + DILATION_STEP : count_of_rows + 2 * DILATION_STEP,
            reverse_column : reverse_column + column_count,
        ]
        weight_change = depth_kernel[2, 2 - column_offset] - depth_kernel[0, column_offset]
        fold_adjustment = fold_adjustment + weight_change[:, None, None] * rim_window.astype(
            jnp.float32
        )
    at_top = lax.axis_index("lat") == lax.axis_size("lat") - 1
    swapped_axes = swapped_axes.at[:, count_of_rows - DILATION_STEP :, :].add(
        jnp.where(at_top, fold_adjustment, jnp.zeros_like(fold_adjustment))
    )
    state_grad = (mask_float * (cotan.astype(jnp.float32) + swapped_axes)).astype(jnp.bfloat16)
    expand_grad, project_grad, bias_grad, kernel_grad = lax.psum(
        (expand_part, project_part, bias_part, kernel_part), ("lon", "lat")
    )
    return (state_grad, expand_grad, project_grad, bias_grad, kernel_grad)


def solution(mesh):
    return jax.shard_map(
        on_device,
        mesh=mesh,
        in_specs=(
            P("ch", "lat", "lon"),
            P("lat", "lon"),
            P("ch", "lat", "lon"),
            P("lat", "lon", None),
            P("lat", "lon", None),
            P(None, None, "ch"),
            P(None, "ch"),
            P("ch"),
            P("ch", None),
        ),
        out_specs=(
            P("ch", "lat", "lon"),
            P(None, "ch"),
            P("ch", None),
            P("ch"),
            P(None, None, "ch"),
        ),
        check_vma=False,
    )
```

profile of v0, /device:TPU:24, one launch (start us, length us, event | category | flops | bytes accessed | tf_op | source)
XLA Modules:
  0.0 1290.9 jit_solution(13573045520863102719)
XLA Ops:
  8.7 1.2 convert_element_type.110
  10.0 3.4 scatter_custom_fusion
  16.0 11.4 collective-permute-start.1
  28.2 1.9 collective-permute-start
  30.1 32.5 %all_gather.13 = bf16[75,2,2048]{2,1,0:T(2,128)(2,1)S(1)} all-gather(bf16[75,2,128]{2,1,0:T(2,128)(2,1)S(1)} %slice.277), channel_id=1, replica_groups=mesh['lon'=16,'lat'=8,'ch'=4] {'lon'}, dimensions={2}, use_global_device_ids=true | all-gather | bytes 652800 | tf_op jit(solution)/shard_map/all_gather | solution.py:30
  63.9 1.1 copy.33
  65.4 3.1 collective-permute-start.2
  69.1 5.5 rev.6
  75.3 4.0 concatenate.54
  79.2 2.8 collective-permute-start.3
  83.0 4.6 collective-permute-done.3
  87.6 1.1 broadcast_select_fusion.1
  88.7 2.4 maximum_maximum_fusion
  91.2 1.1 copy-done.1
  92.8 4.1 fusion.19
  97.1 1.3 dynamic-slice.20
  99.6 2.1 pad.67
  101.8 1.2 copy.42
  103.0 24.7 %all-gather.5.cloned.1.call-done = bf16[300,32,128]{2,1,0:T(8,128)(2,1)} async-done(((bf16[75,32,128]{2,1,0:T(8,128)(2,1)}), bf16[300,32,128]{2,1,0:T(8,128)(2,1)}) %all-gather.5.cloned.1.call-update) | async-done | bytes 2457616 | tf_op jit(solution)/shard_map/all_gather | solution.py:103
  127.6 2.1 pad.68
  129.8 1.2 copy.43
  131.8 1.9 fusion.34
  133.8 2.5 convert_reduce_fusion
  136.3 1.1 copy-done.11
  137.4 1.8 convolution_multiply_fusion
  139.2 2.2 fusion.2
  141.3 28.9 %fusion = bf16[80,4096]{1,0:T(8,128)(2,1)} fusion(bf16[300,4096]{1,0:T(8,128)(2,1)S(1)} %fusion.2), kind=kCustom, calls=%all-reduce-scatter | all-reduce-scatter fusion | flops 1310721 | bytes 3115008
  171.2 1.3 collective-permute-start.8
  173.4 6.0 concatenate.62
  179.4 1.4 constant_dynamic-slice_fusion
  181.2 4.9 fusion.28
  186.4 34.3 %all_gather.15 = bf16[75,2,2048]{2,1,0:T(2,128)(2,1)S(1)} all-gather(bf16[75,2,128]{2,1,0:T(2,128)(2,1)S(1)} %slice.285), channel_id=1, replica_groups=mesh['lon'=16,'lat'=8,'ch'=4] {'lon'}, dimensions={2}, use_global_device_ids=true | all-gather | bytes 652800 | tf_op jit(solution)/shard_map/all_gather | solution.py:30
  222.4 3.3 collective-permute-start.5
  225.7 2.5 collective-permute-start.4
  228.4 4.2 collective-permute-done.4
  235.1 2.9 collective-permute-start.7
  238.1 5.5 rev.7
  244.3 4.0 concatenate.57
  248.3 304.1 %all-reduce.2 = (f32[150]{0:T(256)}, f32[3,3,75]{2,1,0:T(4,128)}) all-reduce(f32[150]{0:T(256)S(1)} %copy-done.33, f32[3,3,75]{2,1,0:T(4,128)S(1)} %maximum_multiply_fusion), channel_id=1, replica_groups=mesh['lon'=16,'lat'=8,'ch'=4] {'lon','lat'}, use_global_device_ids=true, to_apply=%region_5.6 | all-reduce | flops 825 | bytes 6600 | tf_op jit(solution)/shard_map/psum | solution.py:170
  552.4 4.5 collective-permute-start.6
  557.8 2.9 collective-permute-done.6
  560.7 1.1 broadcast_select_fusion
  561.9 2.4 pad_maximum_fusion.1
  564.4 3.4 fusion.24
  568.3 1.1 multiply_convert_fusion.2
  569.4 711.6 %all-reduce.6.cloned.1.call-done = (f32[300,150]{0,1:T(8,128)}, f32[150,300]{1,0:T(8,128)}) async-done(((f32[300,150]{0,1:T(8,128)}, f32[150,300]{1,0:T(8,128)}), (f32[300,150]{0,1:T(8,128)}, f32[150,300]{1,0:T(8,128)})) %all-reduce.6.cloned.1.call-update) | async-done | bytes 360016 | tf_op jit(solution)/shard_map/psum | solution.py:170
  1281.1 1.6 copy.49
  1282.7 1.6 copy.50
  (142 shorter events, 19.9 us)
Async XLA Ops:
  7.2 123.8 %copy-start = (bf16[300,150]{0,1:T(8,128)(2,1)S(1)}, bf16[300,150]{0,1:T(8,128)(2,1)}, u32[]{:S(2)}) copy-start(bf16[300,150]{0,1:T(8,128)(2,1)} %param.19) | copy-start | bytes 270004
  7.2 92.5 %all-gather.3.cloned.1.call-start = ((), (), s32[]{:S(2)}) async-start(), calls=%async_computation | async-start | bytes 3072000 | tf_op jit(solution)/shard_map/all_gather | solution.py:104
  14.4 113.2 %all-gather.5.cloned.1.call-start = ((), (), s32[]{:S(2)}) async-start(), calls=%async_computation.1 | async-start | bytes 3072000 | tf_op jit(solution)/shard_map/all_gather | solution.py:103
  16.0 47.9 %collective-permute-start.1 = (bf16[75,32,2]{0,1,2:T(8,128)(2,1)S(1)}, bf16[75,32,2]{0,1,2:T(8,128)(2,1)S(1)}, u32[]{:S(2)}, u32[]{:S(2)}) collective-permute-start(bf16[75,32,2]{0,1,2:T(8,128)(2,1)S(1)} %copy.31), channel_id=1, source_target_pairs={{32,0},{64,32},{96,64},{128,96},{160,128},{192,160},{224,192},{256... | collective-permute-start | bytes 28808 | tf_op jit(solution)/shard_map/ppermute | solution.py:20
  28.2 34.6 %collective-permute-start = (bf16[75,32,2]{0,1,2:T(8,128)(2,1)S(1)}, bf16[75,32,2]{0,1,2:T(8,128)(2,1)S(1)}, u32[]{:S(2)}, u32[]{:S(2)}) collective-permute-start(bf16[75,32,2]{0,1,2:T(8,128)(2,1)S(1)} %copy.30), channel_id=1, source_target_pairs={{0,32},{32,64},{64,96},{96,128},{128,160},{160,192},{192,224},{224... | collective-permute-start | bytes 28808 | tf_op jit(solution)/shard_map/ppermute | solution.py:17
  63.8 27.3 %copy-start.5 = (bf16[75,32,2]{2,1,0:T(8,128)(2,1)}, bf16[75,32,2]{2,1,0:T(8,128)(2,1)S(1)}, u32[]{:S(2)}) copy-start(bf16[75,32,2]{2,1,0:T(8,128)(2,1)S(1)} %copy.32) | copy-start | bytes 28804
  63.8 4.6 copy-start.13
  64.9 26.2 %copy-start.7 = (bf16[75,32,2]{2,1,0:T(8,128)(2,1)}, bf16[75,32,2]{2,1,0:T(8,128)(2,1)S(1)}, u32[]{:S(2)}) copy-start(bf16[75,32,2]{2,1,0:T(8,128)(2,1)S(1)} %copy.33) | copy-start | bytes 28804
  65.4 16.6 %collective-permute-start.2 = (bf16[75,2,132]{2,1,0:T(2,128)(2,1)S(1)}, bf16[75,2,132]{2,1,0:T(2,128)(2,1)}, u32[]{:S(2)}, u32[]{:S(2)}) collective-permute-start(bf16[75,2,132]{2,1,0:T(2,128)(2,1)S(1)} %get-tuple-element.51), channel_id=1, source_target_pairs={{0,4},{4,8},{8,12},{12,16},{16,20},{20,24},{24,28},{28,0},{1,5},{5... | collective-permute-start | bytes 118808 | tf_op jit(solution)/shard_map/ppermute | solution.py:17
  69.1 22.1 %copy-start.14 = (f32[75]{0:T(128)}, f32[75]{0:T(128)S(1)}, u32[]{:S(2)}) copy-start(f32[75]{0:T(128)S(1)} %get-tuple-element.72) | copy-start | bytes 904
  69.1 22.1 %copy-start.16 = (f32[75]{0:T(128)}, f32[75]{0:T(128)S(1)}, u32[]{:S(2)}) copy-start(f32[75]{0:T(128)S(1)} %get-tuple-element.73) | copy-start | bytes 904
  69.1 22.1 %copy-start.18 = (f32[75]{0:T(128)}, f32[75]{0:T(128)S(1)}, u32[]{:S(2)}) copy-start(f32[75]{0:T(128)S(1)} %get-tuple-element.74) | copy-start | bytes 904
  69.1 22.1 %copy-start.20 = (f32[75]{0:T(128)}, f32[75]{0:T(128)S(1)}, u32[]{:S(2)}) copy-start(f32[75]{0:T(128)S(1)} %get-tuple-element.75) | copy-start | bytes 904
  69.1 22.1 %copy-start.22 = (f32[75]{0:T(128)}, f32[75]{0:T(128)S(1)}, u32[]{:S(2)}) copy-start(f32[75]{0:T(128)S(1)} %get-tuple-element.76) | copy-start | bytes 904
  69.1 22.1 %copy-start.24 = (f32[75]{0:T(128)}, f32[75]{0:T(128)S(1)}, u32[]{:S(2)}) copy-start(f32[75]{0:T(128)S(1)} %get-tuple-element.77) | copy-start | bytes 904
  79.2 8.4 collective-permute-start.3
  88.7 4.1 copy-start.26
  88.7 4.1 copy-start.28
  88.7 4.1 copy-start.30
  96.9 1184.2 %all-reduce.6.cloned.1.call-start = ((), (), s32[]{:S(2)}) async-start(), calls=%async_computation.2 | async-start | bytes 933888 | tf_op jit(solution)/shard_map/psum | solution.py:170
  171.2 2.3 collective-permute-start.8
  172.5 8.5 copy-start.8
  173.4 7.5 copy-start.4
  186.3 41.9 %copy-start.34 = (f32[75]{0:T(128)S(1)}, f32[75]{0:T(128)}, u32[]{:S(2)}) copy-start(f32[75]{0:T(128)} %get-tuple-element.35) | copy-start | bytes 904
  186.3 41.9 %copy-start.35 = (f32[75]{0:T(128)S(1)}, f32[75]{0:T(128)}, u32[]{:S(2)}) copy-start(f32[75]{0:T(128)} %get-tuple-element.36) | copy-start | bytes 904
  186.3 41.9 %copy-start.36 = (f32[75]{0:T(128)S(1)}, f32[75]{0:T(128)}, u32[]{:S(2)}) copy-start(f32[75]{0:T(128)} %get-tuple-element.37) | copy-start | bytes 904
  186.3 41.9 %copy-start.37 = (f32[75]{0:T(128)S(1)}, f32[75]{0:T(128)}, u32[]{:S(2)}) copy-start(f32[75]{0:T(128)} %get-tuple-element.56) | copy-start | bytes 904
  186.4 41.9 %copy-start.38 = (f32[75]{0:T(128)S(1)}, f32[75]{0:T(128)}, u32[]{:S(2)}) copy-start(f32[75]{0:T(128)} %get-tuple-element.57) | copy-start | bytes 904
  186.4 41.9 %copy-start.39 = (f32[75]{0:T(128)S(1)}, f32[75]{0:T(128)}, u32[]{:S(2)}) copy-start(f32[75]{0:T(128)} %get-tuple-element.58) | copy-start | bytes 904
  186.4 42.0 %copy-start.43 = (f32[75]{0:T(128)S(1)}, f32[75]{0:T(128)}, u32[]{:S(2)}) copy-start(f32[75]{0:T(128)} %get-tuple-element.53) | copy-start | bytes 904
  186.4 42.0 %copy-start.44 = (f32[75]{0:T(128)S(1)}, f32[75]{0:T(128)}, u32[]{:S(2)}) copy-start(f32[75]{0:T(128)} %get-tuple-element.54) | copy-start | bytes 904
  186.4 42.0 %copy-start.45 = (f32[75]{0:T(128)S(1)}, f32[75]{0:T(128)}, u32[]{:S(2)}) copy-start(f32[75]{0:T(128)} %get-tuple-element.55) | copy-start | bytes 904
  222.4 11.2 collective-permute-start.5
  225.7 6.8 collective-permute-start.4
  235.1 321.7 %collective-permute-start.7 = (bf16[75,2,132]{2,1,0:T(2,128)(2,1)S(1)}, bf16[75,2,132]{2,1,0:T(2,128)(2,1)}, u32[]{:S(2)}, u32[]{:S(2)}) collective-permute-start(bf16[75,2,132]{2,1,0:T(2,128)(2,1)S(1)} %get-tuple-element.48), channel_id=1, source_target_pairs={{0,4},{4,8},{8,12},{12,16},{16,20},{20,24},{24,28},{28,0},{1,5},{5... | collective-permute-start | bytes 118808 | tf_op jit(solution)/shard_map/ppermute | solution.py:17
  238.1 10.2 copy-start.33
  552.4 8.4 collective-permute-start.6
  561.8 2.5 copy-start.15
  561.8 2.5 copy-start.17
  561.8 2.5 copy-start.19
  561.8 2.5 copy-start.21
  561.8 2.5 copy-start.23
  561.8 2.5 copy-start.25
  561.9 2.5 copy-start.27
  564.4 3.4 copy-start.40
  564.4 3.4 copy-start.41
  564.4 3.4 copy-start.42
  564.4 3.9 copy-start.10
  (11 other events, 18.3 us)
Sparse Core Ops, SparseCore 0:
  14.5 40.5 all-gather.2
  97.0 30.5 all-gather.4
  172.6 1108.3 all-reduce.5
where the time goes:
time: 1290 us
  waiting for transfers between devices  748 us (58%)
  blocking collectives  400 us (31%)
  local copies, waits for them, and re-layouts  52.1 us (4%)
  starting transfers between devices  34 us (3%)
  other arithmetic  32 us (2%)
  between operations  15.4 us (1%)
    psum x1, waiting for transfers between devices, on_device(): lax.psum((expand_part, project_part, bias_part, kernel_part), ('lon', 'la...  712 us
    psum x1, blocking collectives, on_device(): lax.psum((expand_part, project_part, bias_part, kernel_part), ('lon', 'la...  304 us
    all_gather x2, blocking collectives, extend(): gathered = lax.all_gather(uppermost_rows, 'lon', axis=2, tiled=True)  66.9 us
    unnamed x1, blocking collectives  28.9 us
  transfers between devices with their start and end apart: 12, of which 6 were waited for; matrix products, arithmetic and copies ran while one was open for 5% of the time, Pallas kernels for 0%

commit v1 on v0

--- a/solution.py
+++ b/solution.py
@@ -3,57 +3,157 @@
 import jax
 import jax.numpy as jnp
 from jax import lax
+from jax.experimental import pallas as pl
+from jax.experimental.pallas import tpu as pltpu
 from jax.sharding import PartitionSpec as P
 
 DILATION_STEP = 2
 
 
-def with_halo(block, sides, width):
-    for axis, dim in sides:
-        count = lax.axis_size(axis)
-        forward = [(i, i + 1) for i in range(count - 1)]
-        forward.append((count - 1, 0))
-        backward = [(target, source) for source, target in forward]
-        low = lax.ppermute(
-            lax.slice_in_dim(block, block.shape[dim] - width, None, axis=dim), axis, forward
-        )
-        high = lax.ppermute(lax.slice_in_dim(block, 0, width, axis=dim), axis, backward)
-        block = jnp.concatenate([low, block, high], axis=dim)
-    return block
+MESH = pl.DeviceIdType.MESH
+
+
+def ring(count):
+    forward = [(i, (i + 1) % count) for i in range(count)]
+    return forward, [(target, source) for source, target in forward]
 
 
 def extend(ocean_field):
-    count_of_rows = ocean_field.shape[1]
-    column_count = ocean_field.shape[2]
-    halo_padded = with_halo(ocean_field, (("lon", 2), ("lat", 1)), DILATION_STEP)
-    uppermost_rows = ocean_field[:, count_of_rows - DILATION_STEP :, :]
-    gathered = lax.all_gather(uppermost_rows, "lon", axis=2, tiled=True)
-    seam_mirrored = gathered[:, ::-1, ::-1]
-    seam_mirrored = jnp.concatenate(
-        [seam_mirrored[:, :, -DILATION_STEP:], seam_mirrored, seam_mirrored[:, :, :DILATION_STEP]],
-        axis=2,
-    )
-    northern_border = lax.dynamic_slice_in_dim(
-        seam_mirrored, lax.axis_index("lon") * column_count, column_count + 2 * DILATION_STEP, 2
-    )
-    latitude_index = lax.axis_index("lat")
-    southern_boundary = halo_padded[:, :DILATION_STEP, :]
-    southern_border = jnp.where(
-        latitude_index == 0, jnp.zeros_like(southern_boundary), southern_boundary
-    )
-    northern_border = jnp.where(
-        latitude_index == lax.axis_size("lat") - 1,
-        northern_border,
-        halo_padded[:, count_of_rows + DILATION_STEP :, :],
-    )
-    return jnp.concatenate(
+    rows = ocean_field.shape[1]
+    n_lon = lax.axis_size("lon")
+    n_lat = lax.axis_size("lat")
+    east, west = ring(n_lon)
+    low = lax.ppermute(ocean_field[:, :, -DILATION_STEP:], "lon", east)
+    high = lax.ppermute(ocean_field[:, :, :DILATION_STEP], "lon", west)
+    wide = jnp.concatenate([low, ocean_field, high], axis=2)
+    top_rows = wide[:, rows - DILATION_STEP :, :]
+    southern = lax.ppermute(
+        top_rows,
+        ("lon", "lat"),
         [
-            southern_border,
-            halo_padded[:, DILATION_STEP : count_of_rows + DILATION_STEP, :],
-            northern_border,
+            (j * n_lat + i, j * n_lat + i + 1)
+            for i in range(n_lat - 1)
+            for j in range(n_lon)
         ],
-        axis=1,
-    )
+    )
+    at_top = lax.axis_index("lat") == n_lat - 1
+    low_rows = wide[:, :DILATION_STEP, :]
+    northern = lax.ppermute(
+        low_rows,
+        ("lon", "lat"),
+        [
+            (j * n_lat + i + 1, j * n_lat + i)
+            for i in range(n_lat - 1)
+            for j in range(n_lon)
+        ],
+    )
+    mirrored = lax.ppermute(
+        top_rows[:, ::-1, ::-1],
+        ("lon", "lat"),
+        [((n_lon - 1 - j) * n_lat + n_lat - 1, j * n_lat + n_lat - 1) for j in range(n_lon)],
+    )
+    northern = jnp.where(at_top, mirrored, northern)
+    return jnp.concatenate([southern, wide, northern], axis=1)
+
+
+def sum_kernel(first, second, rest, first_out, second_out, rest_out, pad, tiles, whole, lat_in, part, lon_in,
+               send_a, recv_a, send_b, recv_b, send_c, recv_c, send_d, recv_d):
+    n_lat, n_lon = lat_in.shape[0], lon_in.shape[0]
+    lat, lon = lax.axis_index("lat"), lax.axis_index("lon")
+    height, width = first.shape
+    down, across = pad.shape[1] // 8, pad.shape[2] // 128
+
+    def lat_peer(step):
+        return {"lat": lax.rem(lat + step, n_lat)}
+
+    def lon_peer(step):
+        return {"lon": lax.rem(lon + step, n_lon)}
+
+    barrier = pltpu.get_barrier_semaphore()
+    for step in range(1, n_lat):
+        pl.semaphore_signal(barrier, inc=1, device_id=lat_peer(step), device_id_type=MESH)
+    for step in range(1, n_lon):
+        pl.semaphore_signal(barrier, inc=1, device_id=lon_peer(step), device_id_type=MESH)
+
+    pad[...] = jnp.zeros_like(pad)
+    tiles[...] = jnp.zeros_like(tiles)
+    pad[0, :height, :width] = first[...]
+    pad[1, :height, :width] = second[...]
+    spots = [(which, i, j) for which in range(2) for i in range(down) for j in range(across)]
+    for place, (which, i, j) in enumerate(spots):
+        tiles[place // n_lon, place % n_lon] = pad[which, 8 * i : 8 * i + 8, 128 * j : 128 * j + 128]
+    last = len(spots)
+    tiles[last // n_lon, last % n_lon] = rest[...]
+    pl.semaphore_wait(barrier, n_lat + n_lon - 2)
+
+    def exchange(copies):
+        for copy in copies:
+            copy.start()
+        for copy in copies:
+            copy.wait()
+
+    exchange([
+        pltpu.make_async_remote_copy(
+            tiles.at[lax.rem(lat + step, n_lat)], lat_in.at[step], send_a.at[step], recv_a.at[step],
+            device_id=lat_peer(step), device_id_type=MESH)
+        for step in range(1, n_lat)
+    ])
+    total = tiles[lat]
+    for step in range(1, n_lat):
+        total = total + lat_in[step]
+    part[...] = total
+    exchange([
+        pltpu.make_async_remote_copy(
+            part.at[lax.rem(lon + step, n_lon)], lon_in.at[step], send_b.at[step], recv_b.at[step],
+            device_id=lon_peer(step), device_id_type=MESH)
+        for step in range(1, n_lon)
+    ])
+    total = part[lon]
+    for step in range(1, n_lon):
+        total = total + lon_in[step]
+    whole[lat, lon] = total
+    exchange([
+        pltpu.make_async_remote_copy(
+            whole.at[lat, lon], whole.at[lat, lon], send_c.at[step], recv_c.at[step],
+            device_id=lon_peer(step), device_id_type=MESH)
+        for step in range(1, n_lon)
+    ])
+    exchange([
+        pltpu.make_async_remote_copy(
+            whole.at[lat], whole.at[lat], send_d.at[step], recv_d.at[step],
+            device_id=lat_peer(step), device_id_type=MESH)
+        for step in range(1, n_lat)
+    ])
+    for place, (which, i, j) in enumerate(spots):
+        pad[which, 8 * i : 8 * i + 8, 128 * j : 128 * j + 128] = whole[place // n_lon, place % n_lon]
+    first_out[...] = pad[0, :height, :width]
+    second_out[...] = pad[1, :height, :width]
+    rest_out[...] = whole[last // n_lon, last % n_lon]
+
+
+def sum_over_cells(first, second, rest):
+    n_lat, n_lon = lax.axis_size("lat"), lax.axis_size("lon")
+    height, width = first.shape
+    down, across = -(-height // 8), -(-width // 128)
+    vmem = pl.BlockSpec(memory_space=pltpu.VMEM)
+    tile = (8, 128)
+    shapes = [jax.ShapeDtypeStruct(x.shape, x.dtype) for x in (first, second, rest)]
+    return pl.pallas_call(
+        sum_kernel,
+        out_shape=shapes,
+        in_specs=[vmem] * 3,
+        out_specs=[vmem] * 3,
+        scratch_shapes=[
+            pltpu.VMEM((2, 8 * down, 128 * across), jnp.float32),
+            pltpu.VMEM((n_lat, n_lon) + tile, jnp.float32),
+            pltpu.VMEM((n_lat, n_lon) + tile, jnp.float32),
+            pltpu.VMEM((n_lat, n_lon) + tile, jnp.float32),
+            pltpu.VMEM((n_lon,) + tile, jnp.float32),
+            pltpu.VMEM((n_lon,) + tile, jnp.float32),
+        ]
+        + [pltpu.SemaphoreType.DMA((n,)) for n in (n_lat, n_lat, n_lon, n_lon, n_lon, n_lon, n_lat, n_lat)],
+        compiler_params=pltpu.CompilerParams(collective_id=0, has_side_effects=True),
+    )(first, second, rest)
 
 
 def on_device(
@@ -116,7 +216,7 @@
         jnp.dot(activ.astype(jnp.bfloat16), cotan_flat.T, preferred_element_type=jnp.float32)
         * scale
     )
-    expand_part = jnp.dot(conv_flat, pre_grad.T, preferred_element_type=jnp.float32) * scale
+    expand_part = jnp.dot(pre_grad, conv_flat.T, preferred_element_type=jnp.float32) * scale
     bias_part = jnp.sum(pre_grad.astype(jnp.float32), axis=1) * scale
     summed = lax.psum_scatter(
         jnp.dot(expand_weight, pre_grad, preferred_element_type=jnp.float32).astype(jnp.bfloat16),
@@ -167,9 +267,14 @@
         jnp.where(at_top, fold_adjustment, jnp.zeros_like(fold_adjustment))
     )
     state_grad = (mask_float * (cotan.astype(jnp.float32) + swapped_axes)).astype(jnp.bfloat16)
-    expand_grad, project_grad, bias_grad, kernel_grad = lax.psum(
-        (expand_part, project_part, bias_part, kernel_part), ("lon", "lat")
-    )
+    rest = jnp.concatenate([bias_part, kernel_part.reshape(-1)])
+    count = rest.shape[0]
+    rest = jnp.pad(rest, (0, 1024 - count)).reshape(8, 128)
+    expand_sum, project_grad, rest = sum_over_cells(expand_part, project_part, rest)
+    rest = rest.reshape(-1)
+    bias_grad = rest[: bias_part.shape[0]]
+    kernel_grad = rest[bias_part.shape[0] : count].reshape(kernel_part.shape)
+    expand_grad = expand_sum.T
     return (state_grad, expand_grad, project_grad, bias_grad, kernel_grad)
 
 

time: 1290 us -> 246 us (0.19)
  the two profiles are of different devices: /device:TPU:24 before, /device:TPU:6 now
where the time goes in v1:
time: 246 us; the launch traced here: 245 us
  waiting for transfers between devices  52 us (21%)
  starting transfers between devices  40.2 us (16%)
  Pallas kernels  37.6 us (15%)
  local copies, waits for them, and re-layouts  32.4 us (13%)
  blocking collectives  30.5 us (12%)
  other arithmetic  28.7 us (12%)
  between operations  15.7 us (6%)
  matrix products  7.95 us (3%)
    pallas_call x1, Pallas kernels, sum_over_cells(): pl.pallas_call(sum_kernel, out_shape=shapes, in_specs=[vmem] * 3, out_spe...  37.6 us
    unnamed x1, blocking collectives  30.5 us
    all_gather x1, waiting for transfers between devices, on_device(): lax.all_gather(conv_out, 'ch', axis=0, tiled=True)  29 us
    unnamed x111, local copies, waits for them, and re-layouts  21.9 us
    ppermute x2, starting transfers between devices, extend(): high = lax.ppermute(ocean_field[:, :, :DILATION_STEP], 'lon', west)  15.4 us
    ppermute x2, waiting for transfers between devices, extend(): lax.ppermute(top_rows, ('lon', 'lat'), [(j * n_lat + i, j * n_lat + i + 1...  11.4 us
    ppermute x2, starting transfers between devices, extend(): lax.ppermute(low_rows, ('lon', 'lat'), [(j * n_lat + i + 1, j * n_lat + i...  10.1 us
    ppermute x2, starting transfers between devices, extend(): low = lax.ppermute(ocean_field[:, :, -DILATION_STEP:], 'lon', east)  5.74 us
  transfers between devices with their start and end apart: 13, of which 7 were waited for; matrix products, arithmetic and copies ran while one was open for 9% of the time, Pallas kernels for 15%

profile of v1, /device:TPU:6, one launch (start us, length us, event | category | flops | bytes accessed | tf_op | source)
XLA Modules:
  0.0 245.1 jit_solution(10786657948692077252)
XLA Ops:
  7.9 0.8 fusion.49
  8.7 1.2 convert_element_type.112
  10.0 3.4 %scatter_custom_fusion = f32[4096]{0:T(1024)S(1)} fusion(s32[512]{0:T(512)S(1)} %bitcast.110, f32[512]{0:T(512)} %bitcast.111, f32[]{:T(128)} %constant.80.clone.1), kind=kCustom, calls=%fused_computation.86 | custom fusion | flops 512 | bytes 16896 | tf_op jit(solution)/shard_map/scatter-add | solution.py:193
  13.4 1.0 multiply_convert_fusion.3
  16.0 3.8 %collective-permute-start = (bf16[75,32,2]{0,1,2:T(8,128)(2,1)S(1)}, bf16[75,32,2]{0,1,2:T(8,128)(2,1)S(1)}, u32[]{:S(2)}, u32[]{:S(2)}) collective-permute-start(bf16[75,32,2]{0,1,2:T(8,128)(2,1)S(1)} %copy.14), channel_id=1, source_target_pairs={{0,32},{32,64},{64,96},{96,128},{128,160},{160,192},{192,224},{224... | collective-permute-start | bytes 28808 | tf_op jit(solution)/shard_map/ppermute | solution.py:26
  19.8 0.8 copy.15
  20.6 9.5 %collective-permute-start.1 = (bf16[75,32,2]{0,1,2:T(8,128)(2,1)S(1)}, bf16[75,32,2]{0,1,2:T(8,128)(2,1)S(1)}, u32[]{:S(2)}, u32[]{:S(2)}) collective-permute-start(bf16[75,32,2]{0,1,2:T(8,128)(2,1)S(1)} %copy.15), channel_id=1, source_target_pairs={{32,0},{64,32},{96,64},{128,96},{160,128},{192,160},{224,192},{256... | collective-permute-start | bytes 28808 | tf_op jit(solution)/shard_map/ppermute | solution.py:27
  30.1 1.0 copy.16
  31.5 1.0 copy.17
  34.6 5.2 %collective-permute-start.4 = (bf16[75,2,132]{2,1,0:T(2,128)(2,1)S(1)}, bf16[75,2,132]{2,1,0:T(2,128)(2,1)S(1)}, u32[]{:S(2)}, u32[]{:S(2)}) collective-permute-start(bf16[75,2,132]{2,1,0:T(2,128)(2,1)S(1)} %get-tuple-element.53), channel_id=1, source_target_pairs={{4,0},{36,32},{68,64},{100,96},{132,128},{164,160},{196,192},{228,... | collective-permute-start | bytes 118808 | tf_op jit(solution)/shard_map/ppermute | solution.py:41
  39.9 2.1 collective-permute-start.2
  42.0 1.5 collective-permute-done.4
  43.6 6.5 %collective-permute-done.2 = bf16[75,2,132]{2,1,0:T(2,128)(2,1)S(1)} collective-permute-done((bf16[75,2,132]{2,1,0:T(2,128)(2,1)S(1)}, bf16[75,2,132]{2,1,0:T(2,128)(2,1)S(1)}, u32[]{:S(2)}, u32[]{:S(2)}) %collective-permute-start.2) | collective-permute-done | bytes 39632 | tf_op jit(solution)/shard_map/ppermute | solution.py:30
  50.1 2.4 maximum_maximum_fusion
  52.6 1.0 copy-done.1
  54.1 4.1 %fusion.19 = bf16[75,32,128]{2,1,0:T(8,128)(2,1)} fusion(bf16[75,32,128]{2,1,0:T(8,128)(2,1)S(1)} %broadcast_multiply_fusion, f32[75]{0:T(128)S(1)} %get-tuple-element.77, f32[75]{0:T(128)S(1)} %get-tuple-element.78, f32[75]{0:T(128)S(1)} %get-tuple-element.71, f32[75]{0:T(128)S(1)} %get-tuple-element.72, f32[75]{0:T(128)S(1)} %get-tuple-element.73, ...), kind=kLoop, calls=%fused_computation.49 | loop fusion | flops 10137600 | bytes 4937100 | tf_op jit(solution)/shard_map/convert_element_type | solution.py:191
  58.2 1.3 dynamic-slice.20
  60.7 2.1 pad.76
  62.9 1.2 copy.26
  64.1 29.0 %all-gather.5.cloned.1.call-done = bf16[300,32,128]{2,1,0:T(8,128)(2,1)} async-done(((bf16[75,32,128]{2,1,0:T(8,128)(2,1)}), bf16[300,32,128]{2,1,0:T(8,128)(2,1)}) %all-gather.5.cloned.1.call-update) | async-done | bytes 2457616 | tf_op jit(solution)/shard_map/all_gather | solution.py:203
  93.1 2.1 pad.77
  95.2 1.2 copy.27
  96.5 0.8 fusion.1
  97.3 1.9 fusion.34.second
  99.2 2.5 %convert_reduce_fusion = (f32[150]{0:T(256)S(1)}, bf16[150,4096]{1,0:T(8,128)(2,1)S(1)}) fusion(f32[150,4096]{1,0:T(8,128)S(1)} %fusion.1, bf16[300,4096]{1,0:T(8,128)(2,1)S(1)} %bitcast.95, bf16[150,300]{1,0:T(8,128)(2,1)S(1)} %copy-done.47), kind=kOutput, calls=%fused_computation.25 | convolution fusion | flops 382156640 | bytes 6234600 | tf_op jit(solution)/shard_map/dot_general | solution.py:213
  101.8 1.8 convolution_multiply_fusion.first
  103.6 0.9 fusion.2
  104.4 30.5 %fusion = bf16[80,4096]{1,0:T(8,128)(2,1)} fusion(bf16[300,4096]{1,0:T(8,128)(2,1)S(1)} %fusion.2), kind=kCustom, calls=%all-reduce-scatter | all-reduce-scatter fusion | flops 1310721 | bytes 3115008
  134.9 1.0 slice.260
  135.9 2.1 collective-permute-start.10
  138.6 5.1 %collective-permute-done.10 = bf16[15,4096]{1,0:T(8,128)(2,1)S(1)} collective-permute-done((bf16[15,4096]{1,0:T(8,128)(2,1)S(1)}, bf16[15,4096]{1,0:T(8,128)(2,1)S(1)}, u32[]{:S(2)}, u32[]{:S(2)}) %collective-permute-start.10) | collective-permute-done | bytes 122912
  143.7 5.9 %concatenate.58 = bf16[95,4096]{1,0:T(8,128)(2,1)} concatenate(bf16[15,4096]{1,0:T(8,128)(2,1)S(1)} %collective-permute-done.10, bf16[80,4096]{1,0:T(8,128)(2,1)} %fusion), dimensions={0} | concatenate | bytes 1556480
  149.6 1.4 constant_dynamic-slice_fusion
  151.4 4.9 %fusion.28 = (f32[75]{0:T(128)}, f32[75]{0:T(128)}, f32[75]{0:T(128)}, f32[75]{0:T(128)}, f32[75]{0:T(128)}, /*index=5*/f32[75]{0:T(128)}, f32[75]{0:T(128)}, f32[75]{0:T(128)}, f32[75]{0:T(128)}) fusion(bf16[75,32,128]{2,1,0:T(8,128)(2,1)S(1)} %broadcast_multiply_fusion, bf16[75,32,2]{2,1,0:T(8,128)(2,1)S(1)} %copy-done.6, ...), kind=kLoop, calls=%fused_computation.58 | loop fusion | flops 10444125 | bytes 4937100 | tf_op jit(solution)/shard_map/reduce_sum | solution.py:240
  157.3 0.8 copy.21
  158.1 5.9 %collective-permute-start.6 = (bf16[75,32,2]{0,1,2:T(8,128)(2,1)S(1)}, bf16[75,32,2]{0,1,2:T(8,128)(2,1)S(1)}, u32[]{:S(2)}, u32[]{:S(2)}) collective-permute-start(bf16[75,32,2]{0,1,2:T(8,128)(2,1)S(1)} %copy.21), channel_id=1, source_target_pairs={{32,0},{64,32},{96,64},{128,96},{160,128},{192,160},{224,192},{256... | collective-permute-start | bytes 28808 | tf_op jit(solution)/shard_map/ppermute | solution.py:27
  164.1 1.9 collective-permute-start.5
  166.3 4.6 %collective-permute-done.5 = bf16[75,32,2]{0,1,2:T(8,128)(2,1)S(1)} collective-permute-done((bf16[75,32,2]{0,1,2:T(8,128)(2,1)S(1)}, bf16[75,32,2]{0,1,2:T(8,128)(2,1)S(1)}, u32[]{:S(2)}, u32[]{:S(2)}) %collective-permute-start.5) | collective-permute-done | bytes 9632 | tf_op jit(solution)/shard_map/ppermute | solution.py:26
  170.9 1.0 copy.22
  172.0 1.1 copy.23
  175.1 4.9 %collective-permute-start.8 = (bf16[75,2,132]{2,1,0:T(2,128)(2,1)S(1)}, bf16[75,2,132]{2,1,0:T(2,128)(2,1)S(1)}, u32[]{:S(2)}, u32[]{:S(2)}) collective-permute-start(bf16[75,2,132]{2,1,0:T(2,128)(2,1)S(1)} %get-tuple-element.49), channel_id=1, source_target_pairs={{4,0},{36,32},{68,64},{100,96},{132,128},{164,160},{196,192},{228,... | collective-permute-start | bytes 118808 | tf_op jit(solution)/shard_map/ppermute | solution.py:41
  180.7 37.6 %shard_map.128 = (f32[150,300]{1,0:T(8,128)}, f32[150,300]{1,0:T(8,128)}, f32[8,128]{1,0:T(8,128)}) custom-call(f32[150,300]{1,0:T(8,128)} %convolution_multiply_fusion.first, f32[150,300]{1,0:T(8,128)} %fusion.34.second, f32[8,128]{1,0:T(8,128)} %fusion.39.rest), custom_call_target="tpu_custom_call" | custom-call | tf_op jit(solution)/shard_map/pallas_call | solution.py:141
  218.3 1.2 slice.237
  220.9 3.2 %collective-permute-start.9 = (bf16[75,2,132]{2,1,0:T(2,128)(2,1)S(1)}, bf16[75,2,132]{2,1,0:T(2,128)(2,1)S(1)}, u32[]{:S(2)}, u32[]{:S(2)}) collective-permute-start(bf16[75,2,132]{2,1,0:T(2,128)(2,1)S(1)} %get-tuple-element.50), channel_id=1, source_target_pairs={{0,4},{32,36},{64,68},{96,100},{128,132},{160,164},{192,196},{224,... | collective-permute-start | bytes 118808 | tf_op jit(solution)/shard_map/ppermute | solution.py:30
  224.4 4.9 %collective-permute-done.9 = bf16[75,2,132]{2,1,0:T(2,128)(2,1)S(1)} collective-permute-done((bf16[75,2,132]{2,1,0:T(2,128)(2,1)S(1)}, bf16[75,2,132]{2,1,0:T(2,128)(2,1)S(1)}, u32[]{:S(2)}, u32[]{:S(2)}) %collective-permute-start.9) | collective-permute-done | bytes 39632 | tf_op jit(solution)/shard_map/ppermute | solution.py:30
  229.3 2.4 pad_maximum_fusion.1
  231.8 3.4 %fusion.24 = f32[75,32,128]{2,1,0:T(8,128)S(1)} fusion(bf16[75,32,128]{2,1,0:T(8,128)(2,1)S(1)} %slice.261, bf16[75,34,132]{2,1,0:T(8,128)(2,1)S(1)} %get-tuple-element.48, bf16[75,32,2]{2,1,0:T(8,128)(2,1)S(1)} %copy.22, bf16[75,32,2]{2,1,0:T(8,128)(2,1)S(1)} %copy.23, bf16[75,34,132]{2,1,0:T(8,128)(2,1)S(1)} %get-tuple-element.47, f32[75]{0:T(128)S(1)} %copy-done.30, ...), kind=kLoop, calls=%fused_computation.54 | loop fusion | flops 9830400 | bytes 5551500 | tf_op jit(solution)/shard_map/add | solution.py:248
  235.7 1.1 multiply_convert_fusion.2
  (138 shorter events, 14.1 us)
Async XLA Ops:
  7.2 89.3 %copy-start = (bf16[300,150]{0,1:T(8,128)(2,1)S(1)}, bf16[300,150]{0,1:T(8,128)(2,1)}, u32[]{:S(2)}) copy-start(bf16[300,150]{0,1:T(8,128)(2,1)} %param.19) | copy-start | bytes 270004
  7.2 53.6 %all-gather.3.cloned.1.call-start = ((), (), s32[]{:S(2)}) async-start(), calls=%async_computation | async-start | bytes 3072000 | tf_op jit(solution)/shard_map/all_gather | solution.py:204
  14.4 78.7 %all-gather.5.cloned.1.call-start = ((), (), s32[]{:S(2)}) async-start(), calls=%async_computation.1 | async-start | bytes 3072000 | tf_op jit(solution)/shard_map/all_gather | solution.py:203
  16.0 14.1 %collective-permute-start = (bf16[75,32,2]{0,1,2:T(8,128)(2,1)S(1)}, bf16[75,32,2]{0,1,2:T(8,128)(2,1)S(1)}, u32[]{:S(2)}, u32[]{:S(2)}) collective-permute-start(bf16[75,32,2]{0,1,2:T(8,128)(2,1)S(1)} %copy.14), channel_id=1, source_target_pairs={{0,32},{32,64},{64,96},{96,128},{128,160},{160,192},{192,224},{224... | collective-permute-start | bytes 28808 | tf_op jit(solution)/shard_map/ppermute | solution.py:26
  20.6 10.9 %collective-permute-start.1 = (bf16[75,32,2]{0,1,2:T(8,128)(2,1)S(1)}, bf16[75,32,2]{0,1,2:T(8,128)(2,1)S(1)}, u32[]{:S(2)}, u32[]{:S(2)}) collective-permute-start(bf16[75,32,2]{0,1,2:T(8,128)(2,1)S(1)} %copy.15), channel_id=1, source_target_pairs={{32,0},{64,32},{96,64},{128,96},{160,128},{192,160},{224,192},{256... | collective-permute-start | bytes 28808 | tf_op jit(solution)/shard_map/ppermute | solution.py:27
  31.1 21.3 %copy-start.5 = (bf16[75,32,2]{2,1,0:T(8,128)(2,1)}, bf16[75,32,2]{2,1,0:T(8,128)(2,1)S(1)}, u32[]{:S(2)}) copy-start(bf16[75,32,2]{2,1,0:T(8,128)(2,1)S(1)} %copy.16) | copy-start | bytes 28804
  32.6 19.9 %copy-start.7 = (bf16[75,32,2]{2,1,0:T(8,128)(2,1)}, bf16[75,32,2]{2,1,0:T(8,128)(2,1)S(1)}, u32[]{:S(2)}) copy-start(bf16[75,32,2]{2,1,0:T(8,128)(2,1)S(1)} %copy.17) | copy-start | bytes 28804
  32.6 7.2 %copy-start.14 = (f32[3,3,75]{2,1,0:T(4,128)S(1)}, f32[3,3,75]{2,1,0:T(4,128)}, u32[]{:S(2)}) copy-start(f32[3,3,75]{2,1,0:T(4,128)} %param.18) | copy-start | bytes 8104
  33.9 8.1 %collective-permute-start.3 = (bf16[75,2,132]{2,1,0:T(2,128)(2,1)S(1)}, bf16[75,2,132]{2,1,0:T(2,128)(2,1)S(1)}, u32[]{:S(2)}, u32[]{:S(2)}) collective-permute-start(bf16[75,2,132]{2,1,0:T(2,128)(2,1)S(1)} %slice.321), channel_id=1, source_target_pairs={{508,28},{476,60},{444,92},{412,124},{380,156},{348,188},{316,220}... | collective-permute-start | bytes 118808 | tf_op jit(solution)/shard_map/ppermute | solution.py:50
  34.6 8.9 %collective-permute-start.4 = (bf16[75,2,132]{2,1,0:T(2,128)(2,1)S(1)}, bf16[75,2,132]{2,1,0:T(2,128)(2,1)S(1)}, u32[]{:S(2)}, u32[]{:S(2)}) collective-permute-start(bf16[75,2,132]{2,1,0:T(2,128)(2,1)S(1)} %get-tuple-element.53), channel_id=1, source_target_pairs={{4,0},{36,32},{68,64},{100,96},{132,128},{164,160},{196,192},{228,... | collective-permute-start | bytes 118808 | tf_op jit(solution)/shard_map/ppermute | solution.py:41
  39.8 12.7 %copy-start.15 = (f32[75]{0:T(128)}, f32[75]{0:T(128)S(1)}, u32[]{:S(2)}) copy-start(f32[75]{0:T(128)S(1)} %get-tuple-element.70) | copy-start | bytes 904
  39.8 12.7 %copy-start.17 = (f32[75]{0:T(128)}, f32[75]{0:T(128)S(1)}, u32[]{:S(2)}) copy-start(f32[75]{0:T(128)S(1)} %get-tuple-element.71) | copy-start | bytes 904
  39.8 12.7 %copy-start.19 = (f32[75]{0:T(128)}, f32[75]{0:T(128)S(1)}, u32[]{:S(2)}) copy-start(f32[75]{0:T(128)S(1)} %get-tuple-element.72) | copy-start | bytes 904
  39.8 12.7 %copy-start.21 = (f32[75]{0:T(128)}, f32[75]{0:T(128)S(1)}, u32[]{:S(2)}) copy-start(f32[75]{0:T(128)S(1)} %get-tuple-element.73) | copy-start | bytes 904
  39.9 12.7 %copy-start.23 = (f32[75]{0:T(128)}, f32[75]{0:T(128)S(1)}, u32[]{:S(2)}) copy-start(f32[75]{0:T(128)S(1)} %get-tuple-element.74) | copy-start | bytes 904
  39.9 12.7 %copy-start.25 = (f32[75]{0:T(128)}, f32[75]{0:T(128)S(1)}, u32[]{:S(2)}) copy-start(f32[75]{0:T(128)S(1)} %get-tuple-element.75) | copy-start | bytes 904
  39.9 12.7 %copy-start.27 = (f32[75]{0:T(128)}, f32[75]{0:T(128)S(1)}, u32[]{:S(2)}) copy-start(f32[75]{0:T(128)S(1)} %get-tuple-element.76) | copy-start | bytes 904
  39.9 12.7 %copy-start.29 = (f32[75]{0:T(128)}, f32[75]{0:T(128)S(1)}, u32[]{:S(2)}) copy-start(f32[75]{0:T(128)S(1)} %get-tuple-element.77) | copy-start | bytes 904
  39.9 12.7 %copy-start.31 = (f32[75]{0:T(128)}, f32[75]{0:T(128)S(1)}, u32[]{:S(2)}) copy-start(f32[75]{0:T(128)S(1)} %get-tuple-element.78) | copy-start | bytes 904
  39.9 10.1 %collective-permute-start.2 = (bf16[75,2,132]{2,1,0:T(2,128)(2,1)S(1)}, bf16[75,2,132]{2,1,0:T(2,128)(2,1)S(1)}, u32[]{:S(2)}, u32[]{:S(2)}) collective-permute-start(bf16[75,2,132]{2,1,0:T(2,128)(2,1)S(1)} %get-tuple-element.54), channel_id=1, source_target_pairs={{0,4},{32,36},{64,68},{96,100},{128,132},{160,164},{192,196},{224,... | collective-permute-start | bytes 118808 | tf_op jit(solution)/shard_map/ppermute | solution.py:30
  134.9 16.3 %copy-start.8 = (bf16[75,32,2]{2,1,0:T(8,128)(2,1)S(1)}, bf16[75,32,2]{2,1,0:T(8,128)(2,1)}, u32[]{:S(2)}) copy-start(bf16[75,32,2]{2,1,0:T(8,128)(2,1)} %copy-done.7) | copy-start | bytes 28804
  135.9 7.8 %collective-permute-start.10 = (bf16[15,4096]{1,0:T(8,128)(2,1)S(1)}, bf16[15,4096]{1,0:T(8,128)(2,1)S(1)}, u32[]{:S(2)}, u32[]{:S(2)}) collective-permute-start(bf16[15,4096]{1,0:T(8,128)(2,1)S(1)} %slice.260), channel_id=1, source_target_pairs={{0,1},{1,2},{2,3},{4,5},{5,6},{6,7},{8,9},{9,10},{10,11},{12,13},{... | collective-permute-start | bytes 368648
  143.7 7.5 %copy-start.4 = (bf16[75,34,132]{2,1,0:T(8,128)(2,1)S(1)}, bf16[75,34,132]{2,1,0:T(8,128)(2,1)}, u32[]{:S(2)}) copy-start(bf16[75,34,132]{2,1,0:T(8,128)(2,1)} %copy-done.3) | copy-start | bytes 2019604
  156.5 9.5 %copy-start.44 = (f32[75]{0:T(128)S(1)}, f32[75]{0:T(128)}, u32[]{:S(2)}) copy-start(f32[75]{0:T(128)} %get-tuple-element.55) | copy-start | bytes 904
  156.5 9.5 %copy-start.45 = (f32[75]{0:T(128)S(1)}, f32[75]{0:T(128)}, u32[]{:S(2)}) copy-start(f32[75]{0:T(128)} %get-tuple-element.56) | copy-start | bytes 904
  156.5 9.5 %copy-start.46 = (f32[75]{0:T(128)S(1)}, f32[75]{0:T(128)}, u32[]{:S(2)}) copy-start(f32[75]{0:T(128)} %get-tuple-element.57) | copy-start | bytes 904
  156.5 9.5 %copy-start.35 = (f32[75]{0:T(128)S(1)}, f32[75]{0:T(128)}, u32[]{:S(2)}) copy-start(f32[75]{0:T(128)} %get-tuple-element.41) | copy-start | bytes 904
  156.5 9.5 %copy-start.36 = (f32[75]{0:T(128)S(1)}, f32[75]{0:T(128)}, u32[]{:S(2)}) copy-start(f32[75]{0:T(128)} %get-tuple-element.42) | copy-start | bytes 904
  156.5 9.5 %copy-start.37 = (f32[75]{0:T(128)S(1)}, f32[75]{0:T(128)}, u32[]{:S(2)}) copy-start(f32[75]{0:T(128)} %get-tuple-element.43) | copy-start | bytes 904
  156.5 9.5 %copy-start.38 = (f32[75]{0:T(128)S(1)}, f32[75]{0:T(128)}, u32[]{:S(2)}) copy-start(f32[75]{0:T(128)} %get-tuple-element.58) | copy-start | bytes 904
  156.6 9.5 %copy-start.39 = (f32[75]{0:T(128)S(1)}, f32[75]{0:T(128)}, u32[]{:S(2)}) copy-start(f32[75]{0:T(128)} %get-tuple-element.59) | copy-start | bytes 904
  156.6 9.5 %copy-start.40 = (f32[75]{0:T(128)S(1)}, f32[75]{0:T(128)}, u32[]{:S(2)}) copy-start(f32[75]{0:T(128)} %get-tuple-element.60) | copy-start | bytes 904
  158.1 13.8 %collective-permute-start.6 = (bf16[75,32,2]{0,1,2:T(8,128)(2,1)S(1)}, bf16[75,32,2]{0,1,2:T(8,128)(2,1)S(1)}, u32[]{:S(2)}, u32[]{:S(2)}) collective-permute-start(bf16[75,32,2]{0,1,2:T(8,128)(2,1)S(1)} %copy.21), channel_id=1, source_target_pairs={{32,0},{64,32},{96,64},{128,96},{160,128},{192,160},{224,192},{256... | collective-permute-start | bytes 28808 | tf_op jit(solution)/shard_map/ppermute | solution.py:27
  164.1 6.8 %collective-permute-start.5 = (bf16[75,32,2]{0,1,2:T(8,128)(2,1)S(1)}, bf16[75,32,2]{0,1,2:T(8,128)(2,1)S(1)}, u32[]{:S(2)}, u32[]{:S(2)}) collective-permute-start(bf16[75,32,2]{0,1,2:T(8,128)(2,1)S(1)} %copy.20), channel_id=1, source_target_pairs={{0,32},{32,64},{64,96},{96,128},{128,160},{160,192},{192,224},{224... | collective-permute-start | bytes 28808 | tf_op jit(solution)/shard_map/ppermute | solution.py:26
  173.0 7.0 %copy-start.34 = (f32[150]{0:T(256)S(1)}, f32[150]{0:T(256)}, u32[]{:S(2)}) copy-start(f32[150]{0:T(256)} %broadcast_multiply_fusion.1) | copy-start | bytes 1804
  174.4 49.8 %collective-permute-start.7 = (bf16[75,2,132]{2,1,0:T(2,128)(2,1)S(1)}, bf16[75,2,132]{2,1,0:T(2,128)(2,1)S(1)}, u32[]{:S(2)}, u32[]{:S(2)}) collective-permute-start(bf16[75,2,132]{2,1,0:T(2,128)(2,1)S(1)} %slice.322), channel_id=1, source_target_pairs={{508,28},{476,60},{444,92},{412,124},{380,156},{348,188},{316,220}... | collective-permute-start | bytes 118808 | tf_op jit(solution)/shard_map/ppermute | solution.py:50
  175.1 49.1 %collective-permute-start.8 = (bf16[75,2,132]{2,1,0:T(2,128)(2,1)S(1)}, bf16[75,2,132]{2,1,0:T(2,128)(2,1)S(1)}, u32[]{:S(2)}, u32[]{:S(2)}) collective-permute-start(bf16[75,2,132]{2,1,0:T(2,128)(2,1)S(1)} %get-tuple-element.49), channel_id=1, source_target_pairs={{4,0},{36,32},{68,64},{100,96},{132,128},{164,160},{196,192},{228,... | collective-permute-start | bytes 118808 | tf_op jit(solution)/shard_map/ppermute | solution.py:41
  220.9 8.4 %collective-permute-start.9 = (bf16[75,2,132]{2,1,0:T(2,128)(2,1)S(1)}, bf16[75,2,132]{2,1,0:T(2,128)(2,1)S(1)}, u32[]{:S(2)}, u32[]{:S(2)}) collective-permute-start(bf16[75,2,132]{2,1,0:T(2,128)(2,1)S(1)} %get-tuple-element.50), channel_id=1, source_target_pairs={{0,4},{32,36},{64,68},{96,100},{128,132},{160,164},{192,196},{224,... | collective-permute-start | bytes 118808 | tf_op jit(solution)/shard_map/ppermute | solution.py:30
  224.3 7.4 %copy-start.16 = (f32[75]{0:T(128)S(1)}, f32[75]{0:T(128)}, u32[]{:S(2)}) copy-start(f32[75]{0:T(128)} %copy-done.15) | copy-start | bytes 904
  224.3 7.4 %copy-start.18 = (f32[75]{0:T(128)S(1)}, f32[75]{0:T(128)}, u32[]{:S(2)}) copy-start(f32[75]{0:T(128)} %copy-done.17) | copy-start | bytes 904
  224.3 7.4 %copy-start.20 = (f32[75]{0:T(128)S(1)}, f32[75]{0:T(128)}, u32[]{:S(2)}) copy-start(f32[75]{0:T(128)} %copy-done.19) | copy-start | bytes 904
  224.3 7.4 %copy-start.22 = (f32[75]{0:T(128)S(1)}, f32[75]{0:T(128)}, u32[]{:S(2)}) copy-start(f32[75]{0:T(128)} %copy-done.21) | copy-start | bytes 904
  224.3 7.4 %copy-start.24 = (f32[75]{0:T(128)S(1)}, f32[75]{0:T(128)}, u32[]{:S(2)}) copy-start(f32[75]{0:T(128)} %copy-done.23) | copy-start | bytes 904
  224.3 7.4 %copy-start.26 = (f32[75]{0:T(128)S(1)}, f32[75]{0:T(128)}, u32[]{:S(2)}) copy-start(f32[75]{0:T(128)} %copy-done.25) | copy-start | bytes 904
  224.3 7.4 %copy-start.28 = (f32[75]{0:T(128)S(1)}, f32[75]{0:T(128)}, u32[]{:S(2)}) copy-start(f32[75]{0:T(128)} %copy-done.27) | copy-start | bytes 904
  224.4 7.4 %copy-start.30 = (f32[75]{0:T(128)S(1)}, f32[75]{0:T(128)}, u32[]{:S(2)}) copy-start(f32[75]{0:T(128)} %copy-done.29) | copy-start | bytes 904
  224.4 7.4 %copy-start.32 = (f32[75]{0:T(128)S(1)}, f32[75]{0:T(128)}, u32[]{:S(2)}) copy-start(f32[75]{0:T(128)} %copy-done.31) | copy-start | bytes 904
  231.8 3.9 %copy-start.10 = (f32[75,32,128]{2,1,0:T(8,128)S(1)}, f32[75,32,128]{2,1,0:T(8,128)}, u32[]{:S(2)}) copy-start(f32[75,32,128]{2,1,0:T(8,128)} %copy-done.9) | copy-start | bytes 3686404
  (13 other events, 25.4 us)
Sparse Core Ops, SparseCore 0:
  14.5 40.8 all-gather.2
  58.3 34.7 all-gather.4

commit v2 on v0

v2 whole, which is shorter than its diff:
```python
import functools
import math

import jax
import jax.numpy as jnp
from jax import lax
from jax.experimental import pallas as pl
from jax.experimental.pallas import tpu as pltpu
from jax.sharding import PartitionSpec as P

MESH = pl.DeviceIdType.MESH
ROWS = 32
WIDE = 80
LANES = 128
SHARE = 8
UNITS = 160
TILES = 114
REST = 10
BF = jnp.bfloat16
F32 = jnp.float32


def rcopy(src, dst, send, recv, **where):
    return pltpu.make_async_remote_copy(
        src, dst, send, recv, device_id=where, device_id_type=MESH
    )


def three_parts(x):
    high = x.astype(BF)
    left = x - high.astype(F32)
    middle = left.astype(BF)
    low = (left - middle.astype(F32)).astype(BF)
    return high, middle, low


def step_kernel(
    scale, n_lon, n_lat,
    state, grad, mask, offset, value, taps, weights,
    state_out, project_out, expand_out, bias_out, kernel_out,
    fwin, gwin, kb, swath, cotan, conv, cot_all, conv_all, w_all,
    pack_out, pack_in, side, msg_out, msg_in,
    acc_p, acc_e, cg_out, cg_in, tiles, pair_in, cross_in,
    whole, lat_in, part, lon_in, pad,
    es, er, ms, mr, ws, wr, cs, cr, vs, vr, gs, gr, ps, pr, xs, xr,
    send_a, recv_a, send_b, recv_b, send_c, recv_c, send_d, recv_d,
):
    lon, lat, ch = lax.axis_index("lon"), lax.axis_index("lat"), lax.axis_index("ch")
    top = lat == n_lat - 1
    mate = ch + 1 - 2 * lax.rem(ch, 2)
    across = lax.rem(ch + 2, 4)
    mate_across = lax.rem(mate + 2, 4)
    lane = lax.broadcasted_iota(jnp.int32, (WIDE, LANES), 1)

    def lat_peer(step):
        return lax.rem(lat + step, n_lat)

    def lon_peer(step):
        return lax.rem(lon + step, n_lon)

    barrier = pltpu.get_barrier_semaphore()
    for step in range(1, n_lat):
        pl.semaphore_signal(barrier, inc=1, device_id={"lat": lat_peer(step)}, device_id_type=MESH)
    for step in range(1, n_lon):
        pl.semaphore_signal(barrier, inc=1, device_id={"lon": lon_peer(step)}, device_id_type=MESH)
    for step in range(1, 4):
        pl.semaphore_signal(
            barrier, inc=1, device_id={"ch": lax.rem(ch + step, 4)}, device_id_type=MESH
        )

    def pack_edges(use, win):
        def body(r, acc):
            return jnp.where(lane // 4 == r, pltpu.roll(win[1, 2 + r], lax.rem(4 * r + 2, LANES), 1), acc)

        pack_out[use] = lax.fori_loop(0, ROWS, body, jnp.zeros((WIDE, LANES), F32)).astype(BF)

    def edge_copies(use):
        return [
            rcopy(pack_out.at[use], pack_in.at[use, 0], es.at[use, 0], er.at[use, 0], lon=lon_peer(1)),
            rcopy(pack_out.at[use], pack_in.at[use, 1], es.at[use, 1], er.at[use, 1], lon=lon_peer(n_lon - 1)),
        ]

    def send_edges(use):
        for copy in edge_copies(use):
            copy.start()

    def wait_edges(use):
        for copy in edge_copies(use):
            copy.wait()
        side[use] = jnp.where(
            lax.rem(lane, 4) < 2, pack_in[use, 0].astype(F32), pack_in[use, 1].astype(F32)
        )

    north_lat = jnp.minimum(lat + 1, n_lat - 1)
    north_lon = jnp.where(top, n_lon - 1 - lon, lon)
    north_slot = jnp.where(top, 1, 0)
    south_lat = jnp.maximum(lat - 1, 0)

    def north_copy(use):
        return rcopy(
            msg_out.at[use, 1], msg_in.at[use, north_slot], ms.at[use, 1], mr.at[use, north_slot],
            lat=north_lat, lon=north_lon,
        )

    def south_copy(use):
        return rcopy(
            msg_out.at[use, 0], msg_in.at[use, 1], ms.at[use, 0], mr.at[use, 1], lat=south_lat
        )

    def send_rows(use, win):
        edge = side[use]
        msg_out[use, 0, 0] = win[1, 2].astype(BF)
        msg_out[use, 0, 1] = win[1, 3].astype(BF)
        msg_out[use, 0, 2] = edge.astype(BF)

        @pl.when(lat > 0)
        def _():
            south_copy(use).start()

        @pl.when(jnp.logical_not(top))
        def _():
            msg_out[use, 1, 0] = win[1, ROWS].astype(BF)
            msg_out[use, 1, 1] = win[1, ROWS + 1].astype(BF)
            msg_out[use, 1, 2] = edge.astype(BF)

        @pl.when(top)
        def _():
            square = (LANES, LANES)
            turn = (
                lax.broadcasted_iota(jnp.int32, square, 0) + lax.broadcasted_iota(jnp.int32, square, 1)
                == LANES - 1
            ).astype(F32).astype(BF)
            for place, row in enumerate((win[1, ROWS + 1], win[1, ROWS], edge)):
                msg_out[use, 1, place] = jnp.dot(
                    row.astype(BF), turn, preferred_element_type=F32
                ).astype(BF)

        north_copy(use).start()

    def windows(win, p, quad, edge):
        x = win[1, p]
        win[0, p] = jnp.where(lane < 2, pltpu.roll(edge, lax.rem(LANES - 4 * quad, LANES), 1), pltpu.roll(x, 2, 1))
        win[2, p] = jnp.where(
            lane >= LANES - 2,
            pltpu.roll(edge, lax.rem(2 * LANES - 4 - 4 * quad, LANES), 1),
            pltpu.roll(x, LANES - 2, 1),
        )

    def inner_windows(use, win):
        edge = side[use]

        def body(r, unused):
            windows(win, r + 2, r, edge)
            return unused

        lax.fori_loop(0, ROWS, body, 0)

    def wait_rows(use, win):
        @pl.when(lat > 0)
        def _():
            south_copy(use).wait_send()
            rcopy(
                msg_out.at[use, 1], msg_in.at[use, 0], ms.at[use, 1], mr.at[use, 0], lat=south_lat
            ).wait_recv()

        @pl.when(lat == 0)
        def _():
            msg_in[use, 0] = jnp.zeros((3, WIDE, LANES), BF)

        north_copy(use).wait_send()
        rcopy(
            msg_out.at[use, 0], msg_in.at[use, 1], ms.at[use, 0], mr.at[use, 1],
            lat=north_lat, lon=north_lon,
        ).wait_recv()
        for slot, first, quad in ((0, 0, ROWS - 2), (1, ROWS + 2, 0)):
            edge = msg_in[use, slot, 2].astype(F32)
            for t in range(2):
                win[1, first + t] = msg_in[use, slot, t].astype(F32)
                windows(win, first + t, quad + t, edge)

    def scatter(q, src, dst, send, recv):
        @pl.when(ch != q)
        def _():
            rcopy(src, dst, send, recv, ch=jnp.int32(q)).start()

        @pl.when(ch == q)
        def _():
            dst[...] = src[...]

    def settle(q, src, dst, send, recv):
        @pl.when(ch != q)
        def _():
            rcopy(src, dst, send, recv, ch=jnp.int32(q)).wait()

    def masked_rows(r, unused):
        fwin[1, 2 + r] = state[r].astype(F32) * mask[pl.ds(r, 1), :]
        return unused

    lax.fori_loop(0, ROWS, masked_rows, 0)
    pack_edges(0, fwin)
    pl.semaphore_wait(barrier, n_lat + n_lon + 1)
    send_edges(0)

    w_all[ch] = weights[...]
    to_mate = rcopy(weights, w_all.at[ch], ws.at[0], wr.at[0], ch=mate)
    to_across = rcopy(weights, w_all.at[ch], ws.at[1], wr.at[1], ch=across)
    passed = rcopy(w_all.at[across], w_all.at[across], ws.at[2], wr.at[2], ch=mate)
    to_across.start()
    to_mate.start()

    spot = offset[...]
    points = spot.shape[1]
    at_row = (
        lax.broadcasted_iota(jnp.int32, (ROWS, points), 0) == spot // LANES
    ).astype(F32).astype(BF)
    at_col = lax.broadcasted_iota(jnp.int32, (LANES, points), 0) == lax.rem(spot, LANES)
    spread = jnp.where(at_col, value[...], 0.0)
    total = jnp.zeros((ROWS, LANES), F32)
    for piece in three_parts(spread):
        total = total + lax.dot_general(
            at_row, piece, (((1,), (1,)), ((), ())), preferred_element_type=F32
        )
    swath[...] = total * jnp.where(ch == 0, 1.0, 0.0)

    first_channel = lax.broadcasted_iota(jnp.int32, (WIDE, LANES), 0) == 0

    def cotan_rows(r, unused):
        row = grad[r].astype(F32)
        row = row + jnp.where(first_channel, swath[pl.ds(r, 1), :], 0.0)
        cotan[r] = (row * mask[pl.ds(r, 1), :]).astype(BF)
        return unused

    lax.fori_loop(0, ROWS, cotan_rows, 0)
    for q in range(4):
        scatter(q, cotan.at[pl.ds(SHARE * q, SHARE)], cot_all.at[ch], cs.at[q], cr.at[ch])
    for t in range(9):
        kb[t] = jnp.broadcast_to(taps[:, t : t + 1], (WIDE, LANES))

    wait_edges(0)
    send_rows(0, fwin)
    inner_windows(0, fwin)

    def conv_rows(low, high):
        for g in range(WIDE // 16):
            span = slice(16 * g, 16 * g + 16)
            ks = [kb[t, span, :] for t in range(9)]

            def body(r, unused):
                acc = ks[0] * fwin[0, r, span, :]
                for t in range(1, 9):
                    acc = acc + ks[t] * fwin[t % 3, r + 2 * (t // 3), span, :]
                if g == WIDE // 16 - 1:
                    unit = lax.broadcasted_iota(jnp.int32, (16, LANES), 0) + 16 * g
                    acc = jnp.where(unit >= 75, 1.0, acc)
                conv[r, span, :] = acc.astype(BF)
                return unused

            lax.fori_loop(low, high, body, 0)

    def send_conv(q):
        scatter(q, conv.at[pl.ds(SHARE * q, SHARE)], conv_all.at[ch], vs.at[q], vr.at[ch])

    conv_rows(SHARE, 3 * SHARE)
    send_conv(1)
    send_conv(2)
    wait_rows(0, fwin)
    conv_rows(0, SHARE)
    send_conv(0)
    conv_rows(3 * SHARE, 4 * SHARE)
    send_conv(3)

    to_across.wait()
    passed.start()
    to_mate.wait()
    acc_p[...] = jnp.zeros_like(acc_p)
    acc_e[...] = jnp.zeros_like(acc_e)
    rcopy(w_all.at[mate_across], w_all.at[mate_across], ws.at[2], wr.at[2], ch=mate).wait()
    for q in range(4):
        settle(q, cotan.at[pl.ds(SHARE * q, SHARE)], cot_all.at[q], cs.at[q], cr.at[q])
    for q in range(4):
        settle(q, conv.at[pl.ds(SHARE * q, SHARE)], conv_all.at[q], vs.at[q], vr.at[q])

    c0 = math.sqrt(2.0 / math.pi)

    def back_part(c, q):
        return cg_out.at[q, pl.ds(2 * c, 2)]

    def cells(c, unused):
        def both(ref):
            return jnp.concatenate(
                [
                    jnp.concatenate([ref[s, 2 * c + t] for s in range(4)], axis=0)
                    for t in range(2)
                ],
                axis=1,
            )

        x, y = both(conv_all), both(cot_all)
        w1 = w_all[:, 0].reshape(4 * UNITS, 4 * WIDE)
        w2 = w_all[:, 1].reshape(4 * UNITS, 4 * WIDE)
        h = jnp.dot(w1, x, preferred_element_type=F32)
        a = jnp.dot(w2, y, preferred_element_type=F32)
        square = h * h
        t = jnp.tanh(h * (c0 + (c0 * 0.044715) * square))
        half = 0.5 * t + 0.5
        activ = (h * half).astype(BF)
        slope = half + (0.5 * h) * (1.0 - t * t) * (c0 + (3.0 * c0 * 0.044715) * square)
        pre = (a * slope).astype(BF)
        acc_p[...] += lax.dot_general(activ, y, (((1,), (1,)), ((), ())), preferred_element_type=F32)
        acc_e[...] += lax.dot_general(pre, x, (((1,), (1,)), ((), ())), preferred_element_type=F32)
        back = lax.dot_general(w1, pre, (((0,), (0,)), ((), ())), preferred_element_type=F32).astype(BF)
        for q in range(4):
            for t in range(2):
                cg_out[q, 2 * c + t] = back[WIDE * q : WIDE * q + WIDE, LANES * t : LANES * t + LANES]
        for q in range(4):
            scatter(
                q, back_part(c, q), cg_in.at[pl.ds(SHARE * ch + 2 * c, 2)], gs.at[c, q], gr.at[c, ch]
            )
        return unused

    lax.fori_loop(0, SHARE // 2, cells, 0)

    for q in range(4):
        for which, ref in enumerate((acc_p, acc_e)):

            def body(d, unused):
                start = pl.multiple_of(UNITS * q + 8 * d, 8)
                for j in range(3):
                    width = min(LANES, 4 * WIDE - LANES * j)
                    tiles[q, 57 * which + 3 * d + j, :, :width] = ref[pl.ds(start, 8), LANES * j : LANES * j + width]
                    if width < LANES:
                        tiles[q, 57 * which + 3 * d + j, :, width:] = jnp.zeros((8, LANES - width), F32)
                return unused

            lax.fori_loop(0, 19, body, 0)

    used = pl.ds(0, TILES)
    pair = [
        rcopy(tiles.at[mate_across, used], pair_in.at[1], ps.at[1], pr.at[1], ch=mate),
        rcopy(tiles.at[mate, used], pair_in.at[0], ps.at[0], pr.at[0], ch=mate),
    ]
    for copy in pair:
        copy.start()

    for q in range(4):

        def body(c, unused):
            settle(q, back_part(c, q), cg_in.at[pl.ds(SHARE * q + 2 * c, 2)], gs.at[c, q], gr.at[c, q])
            return unused

        lax.fori_loop(0, SHARE // 2, body, 0)

    def grad_rows(r, unused):
        gwin[1, 2 + r] = cg_in[r].astype(F32)
        return unused

    lax.fori_loop(0, ROWS, grad_rows, 0)
    pack_edges(1, gwin)
    send_edges(1)

    def add_tiles(slot, ref):
        def body(d, unused):
            tiles[slot, pl.ds(6 * d, 6)] = tiles[slot, pl.ds(6 * d, 6)] + ref[pl.ds(6 * d, 6)]
            return unused

        lax.fori_loop(0, TILES // 6, body, 0)

    pair[0].wait()
    add_tiles(across, pair_in.at[1])
    cross = rcopy(tiles.at[across, used], cross_in, xs, xr, ch=across)
    cross.start()
    pair[1].wait()
    add_tiles(ch, pair_in.at[0])

    for g in range(REST):
        span = slice(8 * g, 8 * g + 8)

        def body(r, sums):
            now = gwin[1, 2 + r, span, :]
            return tuple(
                sums[t] + now * fwin[t % 3, r + 2 * (t // 3), span, :] for t in range(9)
            )

        sums = lax.fori_loop(0, ROWS, body, tuple(jnp.zeros((8, LANES), F32) for _ in range(9)))
        spots = lax.broadcasted_iota(jnp.int32, (8, LANES), 1)
        kept = jnp.zeros((8, LANES), F32)
        for t in range(9):
            kept = jnp.where(spots == t, jnp.sum(sums[t], axis=1, keepdims=True), kept)
        tiles[ch, TILES + g] = kept
    for g in range(TILES + REST, n_lat * n_lon):
        tiles[ch, g] = jnp.zeros((8, LANES), F32)

    wait_edges(1)
    send_rows(1, gwin)
    cross.wait()
    add_tiles(ch, cross_in)

    def lat_copies():
        return [
            rcopy(tiles.at[ch, pl.ds(n_lon * lat_peer(s), n_lon)], lat_in.at[s], send_a.at[s], recv_a.at[s], lat=lat_peer(s))
            for s in range(1, n_lat)
        ]

    for copy in lat_copies():
        copy.start()

    inner_windows(1, gwin)
    for copy in lat_copies():
        copy.wait()
    total = tiles[ch, pl.ds(n_lon * lat, n_lon)]
    for s in range(1, n_lat):
        total = total + lat_in[s]
    part[...] = total

    def lon_copies():
        return [
            rcopy(part.at[lon_peer(s)], lon_in.at[s], send_b.at[s], recv_b.at[s], lon=lon_peer(s))
            for s in range(1, n_lon)
        ]

    for copy in lon_copies():
        copy.start()

    wait_rows(1, gwin)

    def adjoint_rows(low, high, rim):
        for g in range(WIDE // 16):
            span = slice(16 * g, 16 * g + 16)
            ks = [kb[8 - t, span, :] for t in range(9)]
            if rim:
                for b in range(3):
                    ks[6 + b] = jnp.where(top, kb[6 + b, span, :], ks[6 + b])

            def body(r, unused):
                acc = cotan[r, span, :].astype(F32)
                for t in range(9):
                    acc = acc + ks[t] * gwin[t % 3, r + 2 * (t // 3), span, :]
                state_out[r, span, :] = (acc * mask[pl.ds(r, 1), :]).astype(BF)
                return unused

            lax.fori_loop(low, high, body, 0)

    adjoint_rows(0, ROWS // 2, False)
    for copy in lon_copies():
        copy.wait()
    total = part[lon]
    for s in range(1, n_lon):
        total = total + lon_in[s]
    mine = n_lon * lat + lon
    whole[mine] = total * scale

    def share_lon():
        return [
            rcopy(whole.at[mine], whole.at[mine], send_c.at[s], recv_c.at[s], lon=lon_peer(s))
            for s in range(1, n_lon)
        ]

    for copy in share_lon():
        copy.start()
    adjoint_rows(ROWS // 2, ROWS - 2, False)
    adjoint_rows(ROWS - 2, ROWS, True)
    for s in range(1, n_lon):
        source = n_lon * lat + lon_peer(n_lon - s)
        rcopy(whole.at[source], whole.at[source], send_c.at[s], recv_c.at[s], lon=lon_peer(s)).wait()
    band = pl.ds(n_lon * lat, n_lon)
    for s in range(1, n_lat):
        rcopy(whole.at[band], whole.at[band], send_d.at[s], recv_d.at[s], lat=lat_peer(s)).start()
    for s in range(1, n_lat):
        source = pl.ds(n_lon * lat_peer(n_lat - s), n_lon)
        rcopy(whole.at[source], whole.at[source], send_d.at[s], recv_d.at[s], lat=lat_peer(s)).wait()

    def unpack(d, unused):
        start = pl.multiple_of(8 * d, 8)
        for which in range(2):
            for j in range(3):
                pad[which, pl.ds(start, 8), LANES * j : LANES * j + LANES] = whole[57 * which + 3 * d + j]
        return unused

    lax.fori_loop(0, 19, unpack, 0)
    for q in range(4):
        project_out[:, 75 * q : 75 * q + 75] = pad[0, :150, WIDE * q : WIDE * q + 75]
        expand_out[:, 75 * q : 75 * q + 75] = pad[1, :150, WIDE * q : WIDE * q + 75]
    bias_out[...] = pad[1, :, :LANES]
    for g in range(REST):
        kernel_out[8 * g : 8 * g + 8, :] = whole[TILES + g]


def on_device(
    ocean_state, land_mask, out_grad, swath_offset, swath_value,
    depth_kernel, expand_weight, expand_bias, project_weight,
):
    n_lon, n_lat = lax.axis_size("lon"), lax.axis_size("lat")
    channels = ocean_state.shape[0]
    units = expand_bias.shape[0]
    scale = 1.0 / math.sqrt(ROWS * n_lat * LANES * n_lon)
    extra = WIDE - channels

    def by_rows(x):
        return jnp.pad(jnp.transpose(x, (1, 0, 2)), ((0, 0), (0, extra), (0, 0)))

    taps = jnp.pad(depth_kernel.reshape(9, channels).T, ((0, extra), (0, LANES - 9)))

    def spread(w):
        w = w.reshape(units, 4, channels)
        return jnp.pad(w, ((0, UNITS - units), (0, 0), (0, extra)))

    high = lax.reduce_precision(expand_bias, 8, 7)
    middle = lax.reduce_precision(expand_bias - high, 8, 7)
    low = expand_bias - high - middle
    bias = jnp.stack([high, middle, low], axis=1).astype(BF)
    first = spread(expand_weight.T)
    bias = jnp.pad(bias[:, None, :], ((0, UNITS - units), (0, 3), (channels, extra - 3)))
    first = first + bias
    weights = jnp.stack([first, spread(project_weight)]).reshape(2, UNITS, 4 * WIDE)

    vmem = pl.BlockSpec(memory_space=pltpu.VMEM)
    block = (ROWS, WIDE, LANES)
    all_block = (4, SHARE, WIDE, LANES)
    tile = (8, LANES)
    dma = pltpu.SemaphoreType.DMA
    state, project, expand, bias_grad, kernel_grad = pl.pallas_call(
        functools.partial(step_kernel, scale, n_lon, n_lat),
        out_shape=[
            jax.ShapeDtypeStruct(block, BF),
            jax.ShapeDtypeStruct((units, 4 * channels), F32),
            jax.ShapeDtypeStruct((units, 4 * channels), F32),
            jax.ShapeDtypeStruct((152, LANES), F32),
            jax.ShapeDtypeStruct((WIDE, LANES), F32),
        ],
        in_specs=[vmem] * 7,
        out_specs=[vmem] * 5,
        scratch_shapes=[
            pltpu.VMEM((3, ROWS + 4, WIDE, LANES), F32),
            pltpu.VMEM((3, ROWS + 4, WIDE, LANES), F32),
            pltpu.VMEM((9, WIDE, LANES), F32),
            pltpu.VMEM((ROWS, LANES), F32),
            pltpu.VMEM(block, BF),
            pltpu.VMEM(block, BF),
            pltpu.VMEM(all_block, BF),
            pltpu.VMEM(all_block, BF),
            pltpu.VMEM((4, 2, UNITS, 4 * WIDE), BF),
            pltpu.VMEM((2, WIDE, LANES), BF),
            pltpu.VMEM((2, 2, WIDE, LANES), BF),
            pltpu.VMEM((2, WIDE, LANES), F32),
            pltpu.VMEM((2, 2, 3, WIDE, LANES), BF),
            pltpu.VMEM((2, 2, 3, WIDE, LANES), BF),
            pltpu.VMEM((4 * UNITS, 4 * WIDE), F32),
            pltpu.VMEM((4 * UNITS, 4 * WIDE), F32),
            pltpu.VMEM(all_block, BF),
            pltpu.VMEM(block, BF),
            pltpu.VMEM((4, n_lat * n_lon) + tile, F32),
            pltpu.VMEM((2, TILES) + tile, F32),
            pltpu.VMEM((TILES,) + tile, F32),
            pltpu.VMEM((n_lat * n_lon,) + tile, F32),
            pltpu.VMEM((n_lat, n_lon) + tile, F32),
            pltpu.VMEM((n_lon,) + tile, F32),
            pltpu.VMEM((n_lon,) + tile, F32),
            pltpu.VMEM((2, 152, 3 * LANES), F32),
        ]
        + [dma((2, 2))] * 4
        + [dma((3,))] * 2
        + [dma((4,))] * 4
        + [dma((4, 4))] * 2
        + [dma((2,))] * 2
        + [dma(())] * 2
        + [dma((n_lat,))] * 2
        + [dma((n_lon,))] * 4
        + [dma((n_lat,))] * 2,
        compiler_params=pltpu.CompilerParams(
            collective_id=0, has_side_effects=True, vmem_limit_bytes=56 * 2**20
        ),
    )(
        by_rows(ocean_state),
        by_rows(out_grad),
        land_mask.astype(F32),
        swath_offset.reshape(1, -1),
        swath_value.reshape(1, -1),
        taps,
        weights,
    )
    return (
        jnp.transpose(state[:, :channels], (1, 0, 2)),
        expand.T,
        project,
        bias_grad[:units, channels],
        kernel_grad[:channels, :9].T.reshape(3, 3, channels),
    )


def solution(mesh):
    return jax.shard_map(
        on_device,
        mesh=mesh,
        in_specs=(
            P("ch", "lat", "lon"),
            P("lat", "lon"),
            P("ch", "lat", "lon"),
            P("lat", "lon", None),
            P("lat", "lon", None),
            P(None, None, "ch"),
            P(None, "ch"),
            P("ch"),
            P("ch", None),
        ),
        out_specs=(
            P("ch", "lat", "lon"),
            P(None, "ch"),
            P("ch", None),
            P("ch"),
            P(None, None, "ch"),
        ),
        check_vma=False,
    )
```

time: 1290 us -> 113 us (0.09)
  waiting for transfers between devices: 748 us -> 0 us
  blocking collectives: 400 us -> 0 us
  Pallas kernels: 0 us -> 98.4 us
  local copies, waits for them, and re-layouts: 52.1 us -> 11.7 us
  starting transfers between devices: 34 us -> 0 us
  other arithmetic: 32 us -> 1.6 us
  between operations: 15.4 us -> 0.81 us
    psum x1 -> x0, waiting for transfers between devices: 712 us -> none  [on_device(): lax.psum((expand_part, project_part, bias_part, kernel_part), ('lon', 'la...]
    psum x1 -> x0, blocking collectives: 304 us -> none  [on_device(): lax.psum((expand_part, project_part, bias_part, kernel_part), ('lon', 'la...]
    pallas_call x0 -> x1, Pallas kernels: none -> 98.4 us  [on_device(): pl.pallas_call(functools.partial(step_kernel, scale, n_lon, n_lat), out_s...]
    all_gather x2 -> x0, blocking collectives: 66.9 us -> none  [extend(): gathered = lax.all_gather(uppermost_rows, 'lon', axis=2, tiled=True)]
    ppermute x8 -> x0, starting transfers between devices: 32.4 us -> none  [the longest x4 22 us: with_halo(): lax.ppermute(lax.slice_in_dim(block, 0, width, axis=dim), axis, backward)]
    unnamed x1 -> x0, blocking collectives: 28.9 us -> none
    all_gather x2 -> x0, waiting for transfers between devices: 24.7 us -> none  [the longest x1 24.7 us: on_device(): lax.all_gather(conv_out, 'ch', axis=0, tiled=True)]
    unnamed x105 -> x27, local copies, waits for them, and re-layouts: 23.1 us -> 5.75 us
  transfers between devices with their start and end apart: 12 -> 0, of which waited for: 6 -> 0; matrix products, arithmetic and copies ran while one was open for 5% -> 0% of each run, Pallas kernels for 0% -> 0%
where the time goes in v2:
time: 113 us
  Pallas kernels  98.4 us (87%)
  local copies, waits for them, and re-layouts  11.7 us (10%)
  other arithmetic  1.6 us (1%)
    pallas_call x1, Pallas kernels, on_device(): pl.pallas_call(functools.partial(step_kernel, scale, n_lon, n_lat), out_s...  98.4 us
    unnamed x27, local copies, waits for them, and re-layouts  5.75 us

profile of v2, /device:TPU:24, one launch (start us, length us, event | category | flops | bytes accessed | tf_op | source)
XLA Modules:
  0.0 112.6 jit_solution(16550515939782174543)
XLA Ops:
  0.6 0.0 copy-start.10
  0.6 0.0 copy-start.9
  0.7 0.7 copy-done.10
  1.3 0.0 copy-start.8
  1.4 0.0 copy-done.9
  1.4 0.6 copy-done.8
  2.0 0.0 copy-start.4
  2.0 0.6 convert_element_type.21.mask
  2.6 0.1 copy.36
  2.7 0.6 pad.24.taps
  3.4 0.2 copy.37
  3.6 0.0 copy-done.4
  3.6 0.1 reshape.84
  3.7 0.2 pad_add_fusion
  3.9 0.0 copy-start.5
  4.0 0.1 stack.25
  4.1 0.7 copy-done.5
  4.8 0.1 reshape.85
  5.0 0.0 copy-start
  5.0 0.1 pad.27
  5.1 0.1 stack.26
  5.2 0.7 pad_maximum_fusion.weights
  6.0 0.1 copy-done
  6.1 0.2 copy.43
  6.3 0.0 copy-start.1
  6.3 0.9 pad.22.state
  7.2 0.4 copy-done.1
  7.6 0.2 copy.42
  7.9 0.9 pad.23.grad
  8.8 98.4 %shard_map.128 = (bf16[32,80,128]{2,1,0:T(8,128)(2,1)}, f32[150,300]{1,0:T(8,128)}, f32[150,300]{1,0:T(8,128)}, f32[152,128]{1,0:T(8,128)}, f32[80,128]{1,0:T(8,128)}) custom-call(bf16[32,80,128]{2,1,0:T(8,128)(2,1)} %pad.22.state, bf16[32,80,128]{2,1,0:T(8,128)(2,1)} %pad.23.grad, f32[32,128]{1,0:T(8,128)} %convert_element_type.21.mask, s32[1,512]{1,0:T(1,128)} %bitcast.20, ...), custom_call_target="tpu_custom_call" | custom-call | tf_op jit(solution)/shard_map/pallas_call | solution.py:521
  107.2 1.1 %slice_bitcast_fusion = bf16[75,32,128]{2,0,1:T(8,128)(2,1)S(1)} fusion(bf16[32,80,128]{2,1,0:T(8,128)(2,1)} %get-tuple-element.10), kind=kLoop, calls=%fused_computation.2 | loop fusion | bytes 1228800 | tf_op jit(solution)/shard_map/transpose | solution.py:582
  108.4 0.0 copy-start.6
  108.4 0.0 copy-start.3
  108.4 1.0 copy.39
  109.4 0.0 copy-start.7
  109.4 0.0 copy-done.6
  109.4 0.7 slice_reduce_fusion
  110.1 0.0 copy-done.7
  110.2 0.1 copy.38
  110.2 0.6 reshape.86
  110.9 0.0 copy-done.3
  110.9 0.0 copy-start.2
  110.9 0.7 copy.46
  111.5 0.3 copy-done.2
  111.9 0.7 copy.47
  (7 shorter events, 0.0 us)
Async XLA Ops:
  0.6 0.7 copy-start.10
  0.6 0.7 copy-start.9
  1.3 0.7 copy-start.8
  2.0 1.5 %copy-start.4 = (bf16[300,150]{0,1:T(8,128)(2,1)S(1)}, bf16[300,150]{0,1:T(8,128)(2,1)}, u32[]{:S(2)}) copy-start(bf16[300,150]{0,1:T(8,128)(2,1)} %param.15) | copy-start | bytes 270004
  3.9 0.9 copy-start.5
  5.0 1.1 copy-start
  6.3 1.3 %copy-start.1 = (bf16[75,32,128]{2,1,0:T(8,128)(2,1)S(1)}, bf16[75,32,128]{2,1,0:T(8,128)(2,1)}, u32[]{:S(2)}) copy-start(bf16[75,32,128]{2,1,0:T(8,128)(2,1)} %param.11) | copy-start | bytes 1843204
  108.4 1.0 copy-start.6
  108.4 2.5 %copy-start.3 = (f32[150,300]{1,0:T(8,128)S(1)}, f32[150,300]{1,0:T(8,128)}, u32[]{:S(2)}) copy-start(f32[150,300]{1,0:T(8,128)} %get-tuple-element.11) | copy-start | bytes 540004
  109.4 0.8 copy-start.7
  110.9 1.0 copy-start.2

commit v3 on v2

--- a/solution.py
+++ b/solution.py
@@ -26,6 +26,15 @@
     )
 
 
+def rows_loop(low, high, body, width=4):
+    def several(n, unused):
+        for t in range(width):
+            body(low + n * width + t)
+        return unused
+
+    lax.fori_loop(0, (high - low) // width, several, 0)
+
+
 def three_parts(x):
     high = x.astype(BF)
     left = x - high.astype(F32)
@@ -40,8 +49,8 @@
     state_out, project_out, expand_out, bias_out, kernel_out,
     fwin, gwin, kb, swath, cotan, conv, cot_all, conv_all, w_all,
     pack_out, pack_in, side, msg_out, msg_in,
-    acc_p, acc_e, cg_out, cg_in, tiles, pair_in, cross_in,
-    whole, lat_in, part, lon_in, pad,
+    acc_p, acc_e, cg_out, cg_in, tiles, pair_in, cross_out, cross_in,
+    narrow, lat_in, part, lon_in, band, whole, final, pad,
     es, er, ms, mr, ws, wr, cs, cr, vs, vr, gs, gr, ps, pr, xs, xr,
     send_a, recv_a, send_b, recv_b, send_c, recv_c, send_d, recv_d,
 ):
@@ -70,9 +79,13 @@
 
     def pack_edges(use, win):
         def body(r, acc):
-            return jnp.where(lane // 4 == r, pltpu.roll(win[1, 2 + r], lax.rem(4 * r + 2, LANES), 1), acc)
-
-        pack_out[use] = lax.fori_loop(0, ROWS, body, jnp.zeros((WIDE, LANES), F32)).astype(BF)
+            for t in range(4):
+                row = 4 * r + t
+                moved = pltpu.roll(win[1, 2 + row], lax.rem(4 * row + 2, LANES), 1)
+                acc = jnp.where(lane // 4 == row, moved, acc)
+            return acc
+
+        pack_out[use] = lax.fori_loop(0, ROWS // 4, body, jnp.zeros((WIDE, LANES), F32)).astype(BF)
 
     def edge_copies(use):
         return [
@@ -149,11 +162,7 @@
     def inner_windows(use, win):
         edge = side[use]
 
-        def body(r, unused):
-            windows(win, r + 2, r, edge)
-            return unused
-
-        lax.fori_loop(0, ROWS, body, 0)
+        rows_loop(0, ROWS, lambda r: windows(win, r + 2, r, edge))
 
     def wait_rows(use, win):
         @pl.when(lat > 0)
@@ -192,11 +201,10 @@
         def _():
             rcopy(src, dst, send, recv, ch=jnp.int32(q)).wait()
 
-    def masked_rows(r, unused):
+    def masked_rows(r):
         fwin[1, 2 + r] = state[r].astype(F32) * mask[pl.ds(r, 1), :]
-        return unused
-
-    lax.fori_loop(0, ROWS, masked_rows, 0)
+
+    rows_loop(0, ROWS, masked_rows)
     pack_edges(0, fwin)
     pl.semaphore_wait(barrier, n_lat + n_lon + 1)
     send_edges(0)
@@ -224,13 +232,12 @@
 
     first_channel = lax.broadcasted_iota(jnp.int32, (WIDE, LANES), 0) == 0
 
-    def cotan_rows(r, unused):
+    def cotan_rows(r):
         row = grad[r].astype(F32)
         row = row + jnp.where(first_channel, swath[pl.ds(r, 1), :], 0.0)
         cotan[r] = (row * mask[pl.ds(r, 1), :]).astype(BF)
-        return unused
-
-    lax.fori_loop(0, ROWS, cotan_rows, 0)
+
+    rows_loop(0, ROWS, cotan_rows)
     for q in range(4):
         scatter(q, cotan.at[pl.ds(SHARE * q, SHARE)], cot_all.at[ch], cs.at[q], cr.at[ch])
     for t in range(9):
@@ -239,13 +246,15 @@
     wait_edges(0)
     send_rows(0, fwin)
     inner_windows(0, fwin)
+    to_across.wait()
+    passed.start()
 
     def conv_rows(low, high):
         for g in range(WIDE // 16):
             span = slice(16 * g, 16 * g + 16)
             ks = [kb[t, span, :] for t in range(9)]
 
-            def body(r, unused):
+            def body(r):
                 acc = ks[0] * fwin[0, r, span, :]
                 for t in range(1, 9):
                     acc = acc + ks[t] * fwin[t % 3, r + 2 * (t // 3), span, :]
@@ -253,9 +262,8 @@
                     unit = lax.broadcasted_iota(jnp.int32, (16, LANES), 0) + 16 * g
                     acc = jnp.where(unit >= 75, 1.0, acc)
                 conv[r, span, :] = acc.astype(BF)
-                return unused
-
-            lax.fori_loop(low, high, body, 0)
+
+            rows_loop(low, high, body)
 
     def send_conv(q):
         scatter(q, conv.at[pl.ds(SHARE * q, SHARE)], conv_all.at[ch], vs.at[q], vr.at[ch])
@@ -269,8 +277,6 @@
     conv_rows(3 * SHARE, 4 * SHARE)
     send_conv(3)
 
-    to_across.wait()
-    passed.start()
     to_mate.wait()
     acc_p[...] = jnp.zeros_like(acc_p)
     acc_e[...] = jnp.zeros_like(acc_e)
@@ -306,8 +312,8 @@
         activ = (h * half).astype(BF)
         slope = half + (0.5 * h) * (1.0 - t * t) * (c0 + (3.0 * c0 * 0.044715) * square)
         pre = (a * slope).astype(BF)
-        acc_p[...] += lax.dot_general(activ, y, (((1,), (1,)), ((), ())), preferred_element_type=F32)
-        acc_e[...] += lax.dot_general(pre, x, (((1,), (1,)), ((), ())), preferred_element_type=F32)
+        acc_p[:, : 4 * WIDE] += lax.dot_general(activ, y, (((1,), (1,)), ((), ())), preferred_element_type=F32)
+        acc_e[:, : 4 * WIDE] += lax.dot_general(pre, x, (((1,), (1,)), ((), ())), preferred_element_type=F32)
         back = lax.dot_general(w1, pre, (((0,), (0,)), ((), ())), preferred_element_type=F32).astype(BF)
         for q in range(4):
             for t in range(2):
@@ -326,15 +332,13 @@
             def body(d, unused):
                 start = pl.multiple_of(UNITS * q + 8 * d, 8)
                 for j in range(3):
-                    width = min(LANES, 4 * WIDE - LANES * j)
-                    tiles[q, 57 * which + 3 * d + j, :, :width] = ref[pl.ds(start, 8), LANES * j : LANES * j + width]
-                    if width < LANES:
-                        tiles[q, 57 * which + 3 * d + j, :, width:] = jnp.zeros((8, LANES - width), F32)
+                    place = pl.ds(pl.multiple_of(8 * (57 * which + 3 * d + j), 8), 8)
+                    tiles[q, place, :] = ref[pl.ds(start, 8), LANES * j : LANES * j + LANES]
                 return unused
 
             lax.fori_loop(0, 19, body, 0)
 
-    used = pl.ds(0, TILES)
+    used = pl.ds(0, 8 * TILES)
     pair = [
         rcopy(tiles.at[mate_across, used], pair_in.at[1], ps.at[1], pr.at[1], ch=mate),
         rcopy(tiles.at[mate, used], pair_in.at[0], ps.at[0], pr.at[0], ch=mate),
@@ -350,24 +354,28 @@
 
         lax.fori_loop(0, SHARE // 2, body, 0)
 
-    def grad_rows(r, unused):
+    def grad_rows(r):
         gwin[1, 2 + r] = cg_in[r].astype(F32)
-        return unused
-
-    lax.fori_loop(0, ROWS, grad_rows, 0)
+
+    rows_loop(0, ROWS, grad_rows)
     pack_edges(1, gwin)
     send_edges(1)
 
-    def add_tiles(slot, ref):
+    def add_tiles(slot, ref, out=None):
         def body(d, unused):
-            tiles[slot, pl.ds(6 * d, 6)] = tiles[slot, pl.ds(6 * d, 6)] + ref[pl.ds(6 * d, 6)]
+            place = pl.ds(pl.multiple_of(48 * d, 16), 48)
+            added = tiles[slot, place, :] + ref[place, :].astype(F32)
+            if out is None:
+                tiles[slot, place, :] = added
+            else:
+                out[place, :] = added.astype(BF)
             return unused
 
-        lax.fori_loop(0, TILES // 6, body, 0)
+        lax.fori_loop(0, 8 * TILES // 48, body, 0)
 
     pair[0].wait()
-    add_tiles(across, pair_in.at[1])
-    cross = rcopy(tiles.at[across, used], cross_in, xs, xr, ch=across)
+    add_tiles(across, pair_in.at[1], cross_out)
+    cross = rcopy(cross_out, cross_in, xs, xr, ch=across)
     cross.start()
     pair[1].wait()
     add_tiles(ch, pair_in.at[0])
@@ -375,29 +383,41 @@
     for g in range(REST):
         span = slice(8 * g, 8 * g + 8)
 
-        def body(r, sums):
-            now = gwin[1, 2 + r, span, :]
-            return tuple(
-                sums[t] + now * fwin[t % 3, r + 2 * (t // 3), span, :] for t in range(9)
-            )
-
-        sums = lax.fori_loop(0, ROWS, body, tuple(jnp.zeros((8, LANES), F32) for _ in range(9)))
+        def body(n, sums):
+            for u in range(4):
+                r = 4 * n + u
+                now = gwin[1, 2 + r, span, :]
+                sums = tuple(
+                    sums[t] + now * fwin[t % 3, r + 2 * (t // 3), span, :] for t in range(9)
+                )
+            return sums
+
+        sums = lax.fori_loop(0, ROWS // 4, body, tuple(jnp.zeros((8, LANES), F32) for _ in range(9)))
         spots = lax.broadcasted_iota(jnp.int32, (8, LANES), 1)
         kept = jnp.zeros((8, LANES), F32)
         for t in range(9):
             kept = jnp.where(spots == t, jnp.sum(sums[t], axis=1, keepdims=True), kept)
-        tiles[ch, TILES + g] = kept
-    for g in range(TILES + REST, n_lat * n_lon):
-        tiles[ch, g] = jnp.zeros((8, LANES), F32)
+        tiles[ch, 8 * (TILES + g) : 8 * (TILES + g) + 8, :] = kept
+    spare = 8 * (n_lat * n_lon - TILES - REST)
+    tiles[ch, 8 * (TILES + REST) :, :] = jnp.zeros((spare, LANES), F32)
 
     wait_edges(1)
     send_rows(1, gwin)
     cross.wait()
     add_tiles(ch, cross_in)
+    share = 8 * n_lon
+
+    def lat_share(place):
+        return pl.ds(pl.multiple_of(share * place, 16), share)
+
+    def lon_share(place):
+        return pl.ds(pl.multiple_of(8 * place, 8), 8)
+
+    narrow[...] = tiles[ch].astype(BF)
 
     def lat_copies():
         return [
-            rcopy(tiles.at[ch, pl.ds(n_lon * lat_peer(s), n_lon)], lat_in.at[s], send_a.at[s], recv_a.at[s], lat=lat_peer(s))
+            rcopy(narrow.at[lat_share(lat_peer(s))], lat_in.at[s], send_a.at[s], recv_a.at[s], lat=lat_peer(s))
             for s in range(1, n_lat)
         ]
 
@@ -407,14 +427,14 @@
     inner_windows(1, gwin)
     for copy in lat_copies():
         copy.wait()
-    total = tiles[ch, pl.ds(n_lon * lat, n_lon)]
+    total = tiles[ch, lat_share(lat), :]
     for s in range(1, n_lat):
-        total = total + lat_in[s]
+        total = total + lat_in[s].astype(F32)
     part[...] = total
 
     def lon_copies():
         return [
-            rcopy(part.at[lon_peer(s)], lon_in.at[s], send_b.at[s], recv_b.at[s], lon=lon_peer(s))
+            rcopy(part.at[lon_share(lon_peer(s))], lon_in.at[s], send_b.at[s], recv_b.at[s], lon=lon_peer(s))
             for s in range(1, n_lon)
         ]
 
@@ -431,49 +451,50 @@
                 for b in range(3):
                     ks[6 + b] = jnp.where(top, kb[6 + b, span, :], ks[6 + b])
 
-            def body(r, unused):
+            def body(r):
                 acc = cotan[r, span, :].astype(F32)
                 for t in range(9):
                     acc = acc + ks[t] * gwin[t % 3, r + 2 * (t // 3), span, :]
                 state_out[r, span, :] = (acc * mask[pl.ds(r, 1), :]).astype(BF)
-                return unused
-
-            lax.fori_loop(low, high, body, 0)
+
+            rows_loop(low, high, body, 2)
 
     adjoint_rows(0, ROWS // 2, False)
     for copy in lon_copies():
         copy.wait()
-    total = part[lon]
+    total = part[lon_share(lon), :]
     for s in range(1, n_lon):
         total = total + lon_in[s]
-    mine = n_lon * lat + lon
-    whole[mine] = total * scale
-
-    def share_lon():
-        return [
-            rcopy(whole.at[mine], whole.at[mine], send_c.at[s], recv_c.at[s], lon=lon_peer(s))
-            for s in range(1, n_lon)
-        ]
-
-    for copy in share_lon():
-        copy.start()
+    band[lon_share(lon), :] = total * scale
+
+    def share_lon(s, source):
+        piece = band.at[lon_share(source)]
+        return rcopy(piece, piece, send_c.at[s], recv_c.at[s], lon=lon_peer(s))
+
+    for s in range(1, n_lon):
+        share_lon(s, lon).start()
     adjoint_rows(ROWS // 2, ROWS - 2, False)
     adjoint_rows(ROWS - 2, ROWS, True)
     for s in range(1, n_lon):
-        source = n_lon * lat + lon_peer(n_lon - s)
-        rcopy(whole.at[source], whole.at[source], send_c.at[s], recv_c.at[s], lon=lon_peer(s)).wait()
-    band = pl.ds(n_lon * lat, n_lon)
+        share_lon(s, lon_peer(n_lon - s)).wait()
+    whole[lat_share(lat), :] = band[...].astype(BF)
+
+    def share_lat(s, source):
+        piece = whole.at[lat_share(source)]
+        return rcopy(piece, piece, send_d.at[s], recv_d.at[s], lat=lat_peer(s))
+
     for s in range(1, n_lat):
-        rcopy(whole.at[band], whole.at[band], send_d.at[s], recv_d.at[s], lat=lat_peer(s)).start()
+        share_lat(s, lat).start()
     for s in range(1, n_lat):
-        source = pl.ds(n_lon * lat_peer(n_lat - s), n_lon)
-        rcopy(whole.at[source], whole.at[source], send_d.at[s], recv_d.at[s], lat=lat_peer(s)).wait()
+        share_lat(s, lat_peer(n_lat - s)).wait()
+    final[...] = whole[...].astype(F32)
 
     def unpack(d, unused):
         start = pl.multiple_of(8 * d, 8)
         for which in range(2):
             for j in range(3):
-                pad[which, pl.ds(start, 8), LANES * j : LANES * j + LANES] = whole[57 * which + 3 * d + j]
+                place = pl.ds(pl.multiple_of(8 * (57 * which + 3 * d + j), 8), 8)
+                pad[which, pl.ds(start, 8), LANES * j : LANES * j + LANES] = final[place, :]
         return unused
 
     lax.fori_loop(0, 19, unpack, 0)
@@ -481,8 +502,7 @@
         project_out[:, 75 * q : 75 * q + 75] = pad[0, :150, WIDE * q : WIDE * q + 75]
         expand_out[:, 75 * q : 75 * q + 75] = pad[1, :150, WIDE * q : WIDE * q + 75]
     bias_out[...] = pad[1, :, :LANES]
-    for g in range(REST):
-        kernel_out[8 * g : 8 * g + 8, :] = whole[TILES + g]
+    kernel_out[...] = final[8 * TILES : 8 * (TILES + REST), :]
 
 
 def on_device(
@@ -516,7 +536,7 @@
     vmem = pl.BlockSpec(memory_space=pltpu.VMEM)
     block = (ROWS, WIDE, LANES)
     all_block = (4, SHARE, WIDE, LANES)
-    tile = (8, LANES)
+    all_rows = 8 * n_lat * n_lon
     dma = pltpu.SemaphoreType.DMA
     state, project, expand, bias_grad, kernel_grad = pl.pallas_call(
         functools.partial(step_kernel, scale, n_lon, n_lat),
@@ -544,17 +564,21 @@
             pltpu.VMEM((2, WIDE, LANES), F32),
             pltpu.VMEM((2, 2, 3, WIDE, LANES), BF),
             pltpu.VMEM((2, 2, 3, WIDE, LANES), BF),
-            pltpu.VMEM((4 * UNITS, 4 * WIDE), F32),
-            pltpu.VMEM((4 * UNITS, 4 * WIDE), F32),
+            pltpu.VMEM((4 * UNITS, 3 * LANES), F32),
+            pltpu.VMEM((4 * UNITS, 3 * LANES), F32),
             pltpu.VMEM(all_block, BF),
             pltpu.VMEM(block, BF),
-            pltpu.VMEM((4, n_lat * n_lon) + tile, F32),
-            pltpu.VMEM((2, TILES) + tile, F32),
-            pltpu.VMEM((TILES,) + tile, F32),
-            pltpu.VMEM((n_lat * n_lon,) + tile, F32),
-            pltpu.VMEM((n_lat, n_lon) + tile, F32),
-            pltpu.VMEM((n_lon,) + tile, F32),
-            pltpu.VMEM((n_lon,) + tile, F32),
+            pltpu.VMEM((4, all_rows, LANES), F32),
+            pltpu.VMEM((2, 8 * TILES, LANES), F32),
+            pltpu.VMEM((8 * TILES, LANES), BF),
+            pltpu.VMEM((8 * TILES, LANES), BF),
+            pltpu.VMEM((all_rows, LANES), BF),
+            pltpu.VMEM((n_lat, 8 * n_lon, LANES), BF),
+            pltpu.VMEM((8 * n_lon, LANES), F32),
+            pltpu.VMEM((n_lon, 8, LANES), F32),
+            pltpu.VMEM((8 * n_lon, LANES), F32),
+            pltpu.VMEM((all_rows, LANES), BF),
+            pltpu.VMEM((all_rows, LANES), F32),
             pltpu.VMEM((2, 152, 3 * LANES), F32),
         ]
         + [dma((2, 2))] * 4

time: 113 us -> 102 us (0.903)
  Pallas kernels: 98.4 us -> 87.5 us
    pallas_call x1, Pallas kernels: 98.4 us -> 87.5 us  [on_device(): pl.pallas_call(functools.partial(step_kernel, scale, n_lon, n_lat), out_s...]
where the time goes in v3:
time: 102 us
  Pallas kernels  87.5 us (86%)
  local copies, waits for them, and re-layouts  11.7 us (11%)
  other arithmetic  1.6 us (2%)
    pallas_call x1, Pallas kernels, on_device(): pl.pallas_call(functools.partial(step_kernel, scale, n_lon, n_lat), out_s...  87.5 us
    unnamed x27, local copies, waits for them, and re-layouts  5.75 us

profile of v3, /device:TPU:24, one launch (start us, length us, event | category | flops | bytes accessed | tf_op | source)
XLA Modules:
  0.0 101.6 jit_solution(7781923241030746835)
XLA Ops:
  0.6 0.0 copy-start.10
  0.6 0.0 copy-start.9
  0.7 0.7 copy-done.10
  1.3 0.0 copy-start.8
  1.4 0.0 copy-done.9
  1.4 0.6 copy-done.8
  2.0 0.0 copy-start.4
  2.0 0.6 convert_element_type.21.mask
  2.6 0.1 copy.36
  2.7 0.6 pad.24.taps
  3.4 0.2 copy.37
  3.6 0.0 copy-done.4
  3.6 0.1 reshape.84
  3.7 0.2 pad_add_fusion
  3.9 0.0 copy-start.5
  4.0 0.1 stack.25
  4.1 0.7 copy-done.5
  4.8 0.1 reshape.85
  5.0 0.0 copy-start
  5.0 0.1 pad.27
  5.1 0.1 stack.26
  5.2 0.7 pad_maximum_fusion.weights
  6.0 0.1 copy-done
  6.1 0.2 copy.43
  6.3 0.0 copy-start.1
  6.3 0.9 pad.22.state
  7.2 0.4 copy-done.1
  7.6 0.2 copy.42
  7.9 0.9 pad.23.grad
  8.8 87.5 %shard_map.128 = (bf16[32,80,128]{2,1,0:T(8,128)(2,1)}, f32[150,300]{1,0:T(8,128)}, f32[150,300]{1,0:T(8,128)}, f32[152,128]{1,0:T(8,128)}, f32[80,128]{1,0:T(8,128)}) custom-call(bf16[32,80,128]{2,1,0:T(8,128)(2,1)} %pad.22.state, bf16[32,80,128]{2,1,0:T(8,128)(2,1)} %pad.23.grad, f32[32,128]{1,0:T(8,128)} %convert_element_type.21.mask, s32[1,512]{1,0:T(1,128)} %bitcast.20, ...), custom_call_target="tpu_custom_call" | custom-call | tf_op jit(solution)/shard_map/pallas_call | solution.py:541
  96.3 1.1 %slice_bitcast_fusion = bf16[75,32,128]{2,0,1:T(8,128)(2,1)S(1)} fusion(bf16[32,80,128]{2,1,0:T(8,128)(2,1)} %get-tuple-element.10), kind=kLoop, calls=%fused_computation.2 | loop fusion | bytes 1228800 | tf_op jit(solution)/shard_map/transpose | solution.py:606
  97.4 0.0 copy-start.6
  97.4 0.0 copy-start.3
  97.4 1.0 copy.39
  98.4 0.0 copy-start.7
  98.4 0.0 copy-done.6
  98.4 0.7 slice_reduce_fusion
  99.2 0.0 copy-done.7
  99.2 0.1 copy.38
  99.3 0.6 reshape.86
  99.9 0.0 copy-done.3
  99.9 0.0 copy-start.2
  99.9 0.7 copy.46
  100.6 0.3 copy-done.2
  100.9 0.7 copy.47
  (7 shorter events, 0.0 us)
Async XLA Ops:
  0.6 0.7 copy-start.10
  0.6 0.7 copy-start.9
  1.3 0.7 copy-start.8
  2.0 1.5 %copy-start.4 = (bf16[300,150]{0,1:T(8,128)(2,1)S(1)}, bf16[300,150]{0,1:T(8,128)(2,1)}, u32[]{:S(2)}) copy-start(bf16[300,150]{0,1:T(8,128)(2,1)} %param.15) | copy-start | bytes 270004
  3.9 0.9 copy-start.5
  5.0 1.1 %copy-start = (bf16[75,32,128]{2,1,0:T(8,128)(2,1)S(1)}, bf16[75,32,128]{2,1,0:T(8,128)(2,1)}, u32[]{:S(2)}) copy-start(bf16[75,32,128]{2,1,0:T(8,128)(2,1)} %param.9) | copy-start | bytes 1843204
  6.3 1.3 %copy-start.1 = (bf16[75,32,128]{2,1,0:T(8,128)(2,1)S(1)}, bf16[75,32,128]{2,1,0:T(8,128)(2,1)}, u32[]{:S(2)}) copy-start(bf16[75,32,128]{2,1,0:T(8,128)(2,1)} %param.11) | copy-start | bytes 1843204
  97.4 1.0 copy-start.6
  97.4 2.5 %copy-start.3 = (f32[150,300]{1,0:T(8,128)S(1)}, f32[150,300]{1,0:T(8,128)}, u32[]{:S(2)}) copy-start(f32[150,300]{1,0:T(8,128)} %get-tuple-element.11) | copy-start | bytes 540004
  98.4 0.8 copy-start.7
  99.9 1.0 %copy-start.2 = (f32[150,300]{1,0:T(8,128)S(1)}, f32[150,300]{1,0:T(8,128)}, u32[]{:S(2)}) copy-start(f32[150,300]{1,0:T(8,128)} %get-tuple-element.45) | copy-start | bytes 540004

commit v4 on v3

--- a/solution.py
+++ b/solution.py
@@ -45,11 +45,11 @@
 
 def step_kernel(
     scale, n_lon, n_lat,
-    state, grad, mask, offset, value, taps, weights,
+    state, grad, land, offset, value, taps, weights,
     state_out, project_out, expand_out, bias_out, kernel_out,
-    fwin, gwin, kb, swath, cotan, conv, cot_all, conv_all, w_all,
+    fwin, gwin, kb, mask, tap_rows, swath, cotan, conv, cot_all, conv_all, w_all,
     pack_out, pack_in, side, msg_out, msg_in,
-    acc_p, acc_e, cg_out, cg_in, tiles, pair_in, cross_out, cross_in,
+    acc_p, acc_e, cg_out, cg_in, tiles, pair_out, pair_in, cross_out, cross_in,
     narrow, lat_in, part, lon_in, band, whole, final, pad,
     es, er, ms, mr, ws, wr, cs, cr, vs, vr, gs, gr, ps, pr, xs, xr,
     send_a, recv_a, send_b, recv_b, send_c, recv_c, send_d, recv_d,
@@ -201,20 +201,21 @@
         def _():
             rcopy(src, dst, send, recv, ch=jnp.int32(q)).wait()
 
-    def masked_rows(r):
-        fwin[1, 2 + r] = state[r].astype(F32) * mask[pl.ds(r, 1), :]
-
-    rows_loop(0, ROWS, masked_rows)
-    pack_edges(0, fwin)
-    pl.semaphore_wait(barrier, n_lat + n_lon + 1)
-    send_edges(0)
-
-    w_all[ch] = weights[...]
     to_mate = rcopy(weights, w_all.at[ch], ws.at[0], wr.at[0], ch=mate)
     to_across = rcopy(weights, w_all.at[ch], ws.at[1], wr.at[1], ch=across)
     passed = rcopy(w_all.at[across], w_all.at[across], ws.at[2], wr.at[2], ch=mate)
+    mask[...] = land[...].astype(F32)
+    pl.semaphore_wait(barrier, n_lat + n_lon + 1)
     to_across.start()
     to_mate.start()
+
+    def masked_rows(r):
+        fwin[1, 2 + r] = state[r].astype(F32) * mask[pl.ds(r, 1), :]
+
+    rows_loop(0, ROWS, masked_rows)
+    pack_edges(0, fwin)
+    send_edges(0)
+    w_all[ch] = weights[...]
 
     spot = offset[...]
     points = spot.shape[1]
@@ -240,8 +241,13 @@
     rows_loop(0, ROWS, cotan_rows)
     for q in range(4):
         scatter(q, cotan.at[pl.ds(SHARE * q, SHARE)], cot_all.at[ch], cs.at[q], cr.at[ch])
+    tap_rows[...] = jnp.zeros_like(tap_rows)
+    diagonal = lax.broadcasted_iota(jnp.int32, (WIDE, LANES), 0) == lane
     for t in range(9):
-        kb[t] = jnp.broadcast_to(taps[:, t : t + 1], (WIDE, LANES))
+        tap_rows[t : t + 1, : taps.shape[2]] = taps[t // 3, t % 3 : t % 3 + 1, :]
+    for t in range(9):
+        column = jnp.where(diagonal, tap_rows[t : t + 1, :], 0.0)
+        kb[t] = jnp.broadcast_to(jnp.sum(column, axis=1, keepdims=True), (WIDE, LANES))
 
     wait_edges(0)
     send_rows(0, fwin)
@@ -249,33 +255,34 @@
     to_across.wait()
     passed.start()
 
-    def conv_rows(low, high):
+    def conv_piece(c):
         for g in range(WIDE // 16):
             span = slice(16 * g, 16 * g + 16)
             ks = [kb[t, span, :] for t in range(9)]
-
-            def body(r):
-                acc = ks[0] * fwin[0, r, span, :]
-                for t in range(1, 9):
-                    acc = acc + ks[t] * fwin[t % 3, r + 2 * (t // 3), span, :]
-                if g == WIDE // 16 - 1:
-                    unit = lax.broadcasted_iota(jnp.int32, (16, LANES), 0) + 16 * g
-                    acc = jnp.where(unit >= 75, 1.0, acc)
-                conv[r, span, :] = acc.astype(BF)
-
-            rows_loop(low, high, body)
-
-    def send_conv(q):
-        scatter(q, conv.at[pl.ds(SHARE * q, SHARE)], conv_all.at[ch], vs.at[q], vr.at[ch])
-
-    conv_rows(SHARE, 3 * SHARE)
-    send_conv(1)
-    send_conv(2)
+            for q in range(4):
+                for r in (SHARE * q + 2 * c, SHARE * q + 2 * c + 1):
+                    acc = ks[0] * fwin[0, r, span, :]
+                    for t in range(1, 9):
+                        acc = acc + ks[t] * fwin[t % 3, r + 2 * (t // 3), span, :]
+                    if g == WIDE // 16 - 1:
+                        unit = lax.broadcasted_iota(jnp.int32, (16, LANES), 0) + 16 * g
+                        acc = jnp.where(unit >= 75, 1.0, acc)
+                    conv[r, span, :] = acc.astype(BF)
+
+    def conv_part(c, q):
+        return conv.at[pl.ds(SHARE * q + 2 * c, 2)]
+
+    def send_conv(c):
+        for q in range(4):
+            scatter(q, conv_part(c, q), conv_all.at[ch, pl.ds(2 * c, 2)], vs.at[c, q], vr.at[c, ch])
+
+    for c in (1, 2):
+        conv_piece(c)
+        send_conv(c)
     wait_rows(0, fwin)
-    conv_rows(0, SHARE)
-    send_conv(0)
-    conv_rows(3 * SHARE, 4 * SHARE)
-    send_conv(3)
+    for c in (3, 0):
+        conv_piece(c)
+        send_conv(c)
 
     to_mate.wait()
     acc_p[...] = jnp.zeros_like(acc_p)
@@ -283,15 +290,17 @@
     rcopy(w_all.at[mate_across], w_all.at[mate_across], ws.at[2], wr.at[2], ch=mate).wait()
     for q in range(4):
         settle(q, cotan.at[pl.ds(SHARE * q, SHARE)], cot_all.at[q], cs.at[q], cr.at[q])
-    for q in range(4):
-        settle(q, conv.at[pl.ds(SHARE * q, SHARE)], conv_all.at[q], vs.at[q], vr.at[q])
 
     c0 = math.sqrt(2.0 / math.pi)
 
     def back_part(c, q):
         return cg_out.at[q, pl.ds(2 * c, 2)]
 
-    def cells(c, unused):
+    def cells(n, unused):
+        c = lax.rem(n + 1, 4)
+        for q in range(4):
+            settle(q, conv_part(c, q), conv_all.at[q, pl.ds(2 * c, 2)], vs.at[c, q], vr.at[c, q])
+
         def both(ref):
             return jnp.concatenate(
                 [
@@ -339,9 +348,11 @@
             lax.fori_loop(0, 19, body, 0)
 
     used = pl.ds(0, 8 * TILES)
+    pair_out[1] = tiles[mate_across, used, :].astype(BF)
+    pair_out[0] = tiles[mate, used, :].astype(BF)
     pair = [
-        rcopy(tiles.at[mate_across, used], pair_in.at[1], ps.at[1], pr.at[1], ch=mate),
-        rcopy(tiles.at[mate, used], pair_in.at[0], ps.at[0], pr.at[0], ch=mate),
+        rcopy(pair_out.at[1], pair_in.at[1], ps.at[1], pr.at[1], ch=mate),
+        rcopy(pair_out.at[0], pair_in.at[0], ps.at[0], pr.at[0], ch=mate),
     ]
     for copy in pair:
         copy.start()
@@ -518,7 +529,6 @@
     def by_rows(x):
         return jnp.pad(jnp.transpose(x, (1, 0, 2)), ((0, 0), (0, extra), (0, 0)))
 
-    taps = jnp.pad(depth_kernel.reshape(9, channels).T, ((0, extra), (0, LANES - 9)))
 
     def spread(w):
         w = w.reshape(units, 4, channels)
@@ -554,6 +564,8 @@
             pltpu.VMEM((3, ROWS + 4, WIDE, LANES), F32),
             pltpu.VMEM((9, WIDE, LANES), F32),
             pltpu.VMEM((ROWS, LANES), F32),
+            pltpu.VMEM((16, LANES), F32),
+            pltpu.VMEM((ROWS, LANES), F32),
             pltpu.VMEM(block, BF),
             pltpu.VMEM(block, BF),
             pltpu.VMEM(all_block, BF),
@@ -569,7 +581,8 @@
             pltpu.VMEM(all_block, BF),
             pltpu.VMEM(block, BF),
             pltpu.VMEM((4, all_rows, LANES), F32),
-            pltpu.VMEM((2, 8 * TILES, LANES), F32),
+            pltpu.VMEM((2, 8 * TILES, LANES), BF),
+            pltpu.VMEM((2, 8 * TILES, LANES), BF),
             pltpu.VMEM((8 * TILES, LANES), BF),
             pltpu.VMEM((8 * TILES, LANES), BF),
             pltpu.VMEM((all_rows, LANES), BF),
@@ -583,8 +596,8 @@
         ]
         + [dma((2, 2))] * 4
         + [dma((3,))] * 2
-        + [dma((4,))] * 4
-        + [dma((4, 4))] * 2
+        + [dma((4,))] * 2
+        + [dma((4, 4))] * 4
         + [dma((2,))] * 2
         + [dma(())] * 2
         + [dma((n_lat,))] * 2
@@ -596,10 +609,10 @@
     )(
         by_rows(ocean_state),
         by_rows(out_grad),
-        land_mask.astype(F32),
+        land_mask,
         swath_offset.reshape(1, -1),
         swath_value.reshape(1, -1),
-        taps,
+        depth_kernel,
         weights,
     )
     return (

time: 102 us -> 99 us (0.971)
  Pallas kernels: 87.5 us -> 85.2 us
    pallas_call x1, Pallas kernels: 87.5 us -> 85.2 us  [on_device(): pl.pallas_call(functools.partial(step_kernel, scale, n_lon, n_lat), out_s...]
    unnamed x27 -> x21, local copies, waits for them, and re-layouts: 5.75 us -> 5.12 us
where the time goes in v4:
time: 99 us; the launch traced here: 98.2 us
  Pallas kernels  85.2 us (86%)
  local copies, waits for them, and re-layouts  11.2 us (11%)
  other arithmetic  0.99 us (1%)
    pallas_call x1, Pallas kernels, on_device(): pl.pallas_call(functools.partial(step_kernel, scale, n_lon, n_lat), out_s...  85.2 us
    unnamed x21, local copies, waits for them, and re-layouts  5.12 us

profile of v4, /device:TPU:24, one launch (start us, length us, event | category | flops | bytes accessed | tf_op | source)
XLA Modules:
  0.0 98.2 jit_solution(1697385238140557509)
XLA Ops:
  0.6 0.0 copy-start.7
  0.6 0.7 copy-done.7
  1.4 0.2 copy.33
  1.5 1.0 %reshape.80 = bf16[150,4,75]{2,1,0:T(4,128)(2,1)S(1)} reshape(bf16[150,300]{1,0:T(8,128)(2,1)} %bitcast.17) | data formatting | bytes 180000 | tf_op jit(solution)/shard_map/reshape | solution.py:534
  2.6 0.2 pad_add_fusion
  2.8 0.0 copy-start.4
  2.8 0.1 stack.25
  3.0 0.7 copy-done.4
  3.7 0.1 reshape.81
  3.9 0.0 copy-start
  3.9 0.1 pad.22
  4.0 0.1 stack.26
  4.1 0.7 pad_maximum_fusion.weights
  4.9 0.1 copy-done
  5.0 0.2 copy.39
  5.2 0.0 copy-start.1
  5.2 0.9 pad.18.state
  6.1 0.4 copy-done.1
  6.5 0.2 copy.38
  6.8 0.9 pad.19.grad
  7.7 85.2 %shard_map.128 = (bf16[32,80,128]{2,1,0:T(8,128)(2,1)}, f32[150,300]{1,0:T(8,128)}, f32[150,300]{1,0:T(8,128)}, f32[152,128]{1,0:T(8,128)}, f32[80,128]{1,0:T(8,128)}) custom-call(bf16[32,80,128]{2,1,0:T(8,128)(2,1)} %pad.18.state, bf16[32,80,128]{2,1,0:T(8,128)(2,1)} %pad.19.grad, s32[32,128]{1,0:T(8,128)} %land.1, s32[1,512]{1,0:T(1,128)} %bitcast.18, ...), custom_call_target="tpu_custom_call" | custom-call | tf_op jit(solution)/shard_map/pallas_call | solution.py:551
  92.9 1.1 %slice_bitcast_fusion = bf16[75,32,128]{2,0,1:T(8,128)(2,1)S(1)} fusion(bf16[32,80,128]{2,1,0:T(8,128)(2,1)} %get-tuple-element.10), kind=kLoop, calls=%fused_computation.2 | loop fusion | bytes 1228800 | tf_op jit(solution)/shard_map/transpose | solution.py:619
  94.0 0.0 copy-start.5
  94.1 0.0 copy-start.3
  94.1 1.0 %copy.35 = bf16[75,32,128]{2,1,0:T(8,128)(2,1)} copy(bf16[75,32,128]{2,0,1:T(8,128)(2,1)S(1)} %slice_bitcast_fusion) | data formatting | bytes 1228800
  95.0 0.0 copy-start.6
  95.1 0.0 copy-done.5
  95.1 0.7 slice_reduce_fusion
  95.8 0.0 copy-done.6
  95.8 0.1 copy.34
  95.9 0.6 reshape.82
  96.5 0.0 copy-done.3
  96.5 0.0 copy-start.2
  96.5 0.7 copy.42
  97.2 0.3 copy-done.2
  97.6 0.7 copy.43
  (6 shorter events, 0.0 us)
Async XLA Ops:
  0.6 0.7 copy-start.7
  2.8 0.9 copy-start.4
  3.9 1.1 %copy-start = (bf16[75,32,128]{2,1,0:T(8,128)(2,1)S(1)}, bf16[75,32,128]{2,1,0:T(8,128)(2,1)}, u32[]{:S(2)}) copy-start(bf16[75,32,128]{2,1,0:T(8,128)(2,1)} %param.9) | copy-start | bytes 1843204
  5.2 1.3 %copy-start.1 = (bf16[75,32,128]{2,1,0:T(8,128)(2,1)S(1)}, bf16[75,32,128]{2,1,0:T(8,128)(2,1)}, u32[]{:S(2)}) copy-start(bf16[75,32,128]{2,1,0:T(8,128)(2,1)} %param.11) | copy-start | bytes 1843204
  94.0 1.0 %copy-start.5 = (f32[152,128]{1,0:T(8,128)S(1)}, f32[152,128]{1,0:T(8,128)}, u32[]{:S(2)}) copy-start(f32[152,128]{1,0:T(8,128)} %get-tuple-element.13) | copy-start | bytes 233476
  94.1 2.5 %copy-start.3 = (f32[150,300]{1,0:T(8,128)S(1)}, f32[150,300]{1,0:T(8,128)}, u32[]{:S(2)}) copy-start(f32[150,300]{1,0:T(8,128)} %get-tuple-element.11) | copy-start | bytes 540004
  95.0 0.8 copy-start.6
  96.5 1.0 %copy-start.2 = (f32[150,300]{1,0:T(8,128)S(1)}, f32[150,300]{1,0:T(8,128)}, u32[]{:S(2)}) copy-start(f32[150,300]{1,0:T(8,128)} %get-tuple-element.45) | copy-start | bytes 540004

commit v5 on v4

--- a/solution.py
+++ b/solution.py
@@ -59,6 +59,7 @@
     mate = ch + 1 - 2 * lax.rem(ch, 2)
     across = lax.rem(ch + 2, 4)
     mate_across = lax.rem(mate + 2, 4)
+    far = lax.rem(lat + n_lat // 2, n_lat)
     lane = lax.broadcasted_iota(jnp.int32, (WIDE, LANES), 1)
 
     def lat_peer(step):
@@ -76,6 +77,9 @@
         pl.semaphore_signal(
             barrier, inc=1, device_id={"ch": lax.rem(ch + step, 4)}, device_id_type=MESH
         )
+    pl.semaphore_signal(
+        barrier, inc=1, device_id={"ch": across, "lat": far}, device_id_type=MESH
+    )
 
     def pack_edges(use, win):
         def body(r, acc):
@@ -202,10 +206,10 @@
             rcopy(src, dst, send, recv, ch=jnp.int32(q)).wait()
 
     to_mate = rcopy(weights, w_all.at[ch], ws.at[0], wr.at[0], ch=mate)
-    to_across = rcopy(weights, w_all.at[ch], ws.at[1], wr.at[1], ch=across)
+    to_across = rcopy(weights, w_all.at[ch], ws.at[1], wr.at[1], ch=across, lat=far)
     passed = rcopy(w_all.at[across], w_all.at[across], ws.at[2], wr.at[2], ch=mate)
     mask[...] = land[...].astype(F32)
-    pl.semaphore_wait(barrier, n_lat + n_lon + 1)
+    pl.semaphore_wait(barrier, n_lat + n_lon + 2)
     to_across.start()
     to_mate.start()
 
@@ -386,7 +390,7 @@
 
     pair[0].wait()
     add_tiles(across, pair_in.at[1], cross_out)
-    cross = rcopy(cross_out, cross_in, xs, xr, ch=across)
+    cross = rcopy(cross_out, cross_in, xs, xr, ch=across, lat=far)
     cross.start()
     pair[1].wait()
     add_tiles(ch, pair_in.at[0])

time: 99 us -> 99 us (level)
  no operation moved by 1% of the time
where the time goes in v5:
time: 99 us; the launch traced here: 98.2 us
  Pallas kernels  85.2 us (86%)
  local copies, waits for them, and re-layouts  11.2 us (11%)
  other arithmetic  0.99 us (1%)
    pallas_call x1, Pallas kernels, on_device(): pl.pallas_call(functools.partial(step_kernel, scale, n_lon, n_lat), out_s...  85.2 us
    unnamed x21, local copies, waits for them, and re-layouts  5.12 us

profile of v5, /device:TPU:24, one launch (start us, length us, event | category | flops | bytes accessed | tf_op | source)
XLA Modules:
  0.0 98.2 jit_solution(12423653582653364965)
XLA Ops:
  0.6 0.0 copy-start.7
  0.6 0.7 copy-done.7
  1.4 0.2 copy.33
  1.5 1.0 %reshape.80 = bf16[150,4,75]{2,1,0:T(4,128)(2,1)S(1)} reshape(bf16[150,300]{1,0:T(8,128)(2,1)} %bitcast.17) | data formatting | bytes 180000 | tf_op jit(solution)/shard_map/reshape | solution.py:538
  2.6 0.2 pad_add_fusion
  2.8 0.0 copy-start.4
  2.8 0.1 stack.25
  3.0 0.7 copy-done.4
  3.7 0.1 reshape.81
  3.9 0.0 copy-start
  3.9 0.1 pad.22
  4.0 0.1 stack.26
  4.1 0.7 pad_maximum_fusion.weights
  4.9 0.1 copy-done
  5.0 0.2 copy.39
  5.2 0.0 copy-start.1
  5.2 0.9 pad.18.state
  6.1 0.4 copy-done.1
  6.5 0.2 copy.38
  6.8 0.9 pad.19.grad
  7.7 85.2 %shard_map.128 = (bf16[32,80,128]{2,1,0:T(8,128)(2,1)}, f32[150,300]{1,0:T(8,128)}, f32[150,300]{1,0:T(8,128)}, f32[152,128]{1,0:T(8,128)}, f32[80,128]{1,0:T(8,128)}) custom-call(bf16[32,80,128]{2,1,0:T(8,128)(2,1)} %pad.18.state, bf16[32,80,128]{2,1,0:T(8,128)(2,1)} %pad.19.grad, s32[32,128]{1,0:T(8,128)} %land.1, s32[1,512]{1,0:T(1,128)} %bitcast.18, ...), custom_call_target="tpu_custom_call" | custom-call | tf_op jit(solution)/shard_map/pallas_call | solution.py:555
  92.9 1.1 %slice_bitcast_fusion = bf16[75,32,128]{2,0,1:T(8,128)(2,1)S(1)} fusion(bf16[32,80,128]{2,1,0:T(8,128)(2,1)} %get-tuple-element.10), kind=kLoop, calls=%fused_computation.2 | loop fusion | bytes 1228800 | tf_op jit(solution)/shard_map/transpose | solution.py:623
  94.0 0.0 copy-start.5
  94.0 0.0 copy-start.3
  94.1 1.0 %copy.35 = bf16[75,32,128]{2,1,0:T(8,128)(2,1)} copy(bf16[75,32,128]{2,0,1:T(8,128)(2,1)S(1)} %slice_bitcast_fusion) | data formatting | bytes 1228800
  95.0 0.0 copy-start.6
  95.0 0.0 copy-done.5
  95.0 0.7 slice_reduce_fusion
  95.8 0.0 copy-done.6
  95.8 0.1 copy.34
  95.9 0.6 reshape.82
  96.5 0.0 copy-done.3
  96.5 0.0 copy-start.2
  96.5 0.7 copy.42
  97.2 0.3 copy-done.2
  97.5 0.7 copy.43
  (6 shorter events, 0.0 us)
Async XLA Ops:
  0.6 0.7 copy-start.7
  2.8 0.9 copy-start.4
  3.9 1.1 %copy-start = (bf16[75,32,128]{2,1,0:T(8,128)(2,1)S(1)}, bf16[75,32,128]{2,1,0:T(8,128)(2,1)}, u32[]{:S(2)}) copy-start(bf16[75,32,128]{2,1,0:T(8,128)(2,1)} %param.9) | copy-start | bytes 1843204
  5.2 1.3 %copy-start.1 = (bf16[75,32,128]{2,1,0:T(8,128)(2,1)S(1)}, bf16[75,32,128]{2,1,0:T(8,128)(2,1)}, u32[]{:S(2)}) copy-start(bf16[75,32,128]{2,1,0:T(8,128)(2,1)} %param.11) | copy-start | bytes 1843204
  94.0 1.0 %copy-start.5 = (f32[152,128]{1,0:T(8,128)S(1)}, f32[152,128]{1,0:T(8,128)}, u32[]{:S(2)}) copy-start(f32[152,128]{1,0:T(8,128)} %get-tuple-element.13) | copy-start | bytes 233476
  94.0 2.5 %copy-start.3 = (f32[150,300]{1,0:T(8,128)S(1)}, f32[150,300]{1,0:T(8,128)}, u32[]{:S(2)}) copy-start(f32[150,300]{1,0:T(8,128)} %get-tuple-element.11) | copy-start | bytes 540004
  95.0 0.8 copy-start.6
  96.5 1.0 %copy-start.2 = (f32[150,300]{1,0:T(8,128)S(1)}, f32[150,300]{1,0:T(8,128)}, u32[]{:S(2)}) copy-start(f32[150,300]{1,0:T(8,128)} %get-tuple-element.45) | copy-start | bytes 540004

commit v6 on v5

--- a/solution.py
+++ b/solution.py
@@ -45,9 +45,9 @@
 
 def step_kernel(
     scale, n_lon, n_lat,
-    state, grad, land, offset, value, taps, weights,
+    state, grad, land, offset, value, taps, expand, project, bias,
     state_out, project_out, expand_out, bias_out, kernel_out,
-    fwin, gwin, kb, mask, tap_rows, swath, cotan, conv, cot_all, conv_all, w_all,
+    spread_out, weights, bias_row, turned, fwin, gwin, kb, mask, tap_rows, swath, cotan, conv, cot_all, conv_all, w_all,
     pack_out, pack_in, side, msg_out, msg_in,
     acc_p, acc_e, cg_out, cg_in, tiles, pair_out, pair_in, cross_out, cross_in,
     narrow, lat_in, part, lon_in, band, whole, final, pad,
@@ -210,8 +210,6 @@
     passed = rcopy(w_all.at[across], w_all.at[across], ws.at[2], wr.at[2], ch=mate)
     mask[...] = land[...].astype(F32)
     pl.semaphore_wait(barrier, n_lat + n_lon + 2)
-    to_across.start()
-    to_mate.start()
 
     def masked_rows(r):
         fwin[1, 2 + r] = state[r].astype(F32) * mask[pl.ds(r, 1), :]
@@ -219,7 +217,6 @@
     rows_loop(0, ROWS, masked_rows)
     pack_edges(0, fwin)
     send_edges(0)
-    w_all[ch] = weights[...]
 
     spot = offset[...]
     points = spot.shape[1]
@@ -245,6 +242,23 @@
     rows_loop(0, ROWS, cotan_rows)
     for q in range(4):
         scatter(q, cotan.at[pl.ds(SHARE * q, SHARE)], cot_all.at[ch], cs.at[q], cr.at[ch])
+    units, channels = project.shape[0], project.shape[1] // 4
+    spread_out[...] = jnp.zeros_like(spread_out)
+    bias_row[...] = jnp.zeros_like(bias_row)
+    bias_row[0:1, :units] = bias[...]
+    for which, ref in enumerate((expand, project)):
+        full = ref[...].astype(F32)
+        for q in range(4):
+            spread_out[which, :units, WIDE * q : WIDE * q + channels] = full[:, channels * q : channels * q + channels]
+    grid = (UNITS, 2 * LANES)
+    same = lax.broadcasted_iota(jnp.int32, grid, 0) == lax.broadcasted_iota(jnp.int32, grid, 1)
+    column = jnp.sum(jnp.where(same, bias_row[0:1, :], 0.0), axis=1, keepdims=True)
+    for place, piece in enumerate(three_parts(column)):
+        spread_out[0, :, channels + place : channels + place + 1] = piece.astype(F32)
+    weights[...] = spread_out[:, :, : 4 * WIDE].astype(BF)
+    to_across.start()
+    to_mate.start()
+    w_all[ch] = weights[...]
     tap_rows[...] = jnp.zeros_like(tap_rows)
     diagonal = lax.broadcasted_iota(jnp.int32, (WIDE, LANES), 0) == lane
     for t in range(9):
@@ -516,8 +530,13 @@
     for q in range(4):
         project_out[:, 75 * q : 75 * q + 75] = pad[0, :150, WIDE * q : WIDE * q + 75]
         expand_out[:, 75 * q : 75 * q + 75] = pad[1, :150, WIDE * q : WIDE * q + 75]
-    bias_out[...] = pad[1, :, :LANES]
-    kernel_out[...] = final[8 * TILES : 8 * (TILES + REST), :]
+    turned[...] = jnp.zeros_like(turned)
+    turned[:152, :] = pad[1, :, :LANES]
+    turned[2 * LANES : 2 * LANES + WIDE, :] = final[8 * TILES : 8 * (TILES + REST), :]
+    flipped = jnp.transpose(turned[...])
+    bias_out[...] = flipped[channels : channels + 1, :units]
+    for t in range(9):
+        kernel_out[t // 3, t % 3 : t % 3 + 1, :] = flipped[t : t + 1, 2 * LANES : 2 * LANES + channels]
 
 
 def on_device(
@@ -533,19 +552,6 @@
     def by_rows(x):
         return jnp.pad(jnp.transpose(x, (1, 0, 2)), ((0, 0), (0, extra), (0, 0)))
 
-
-    def spread(w):
-        w = w.reshape(units, 4, channels)
-        return jnp.pad(w, ((0, UNITS - units), (0, 0), (0, extra)))
-
-    high = lax.reduce_precision(expand_bias, 8, 7)
-    middle = lax.reduce_precision(expand_bias - high, 8, 7)
-    low = expand_bias - high - middle
-    bias = jnp.stack([high, middle, low], axis=1).astype(BF)
-    first = spread(expand_weight.T)
-    bias = jnp.pad(bias[:, None, :], ((0, UNITS - units), (0, 3), (channels, extra - 3)))
-    first = first + bias
-    weights = jnp.stack([first, spread(project_weight)]).reshape(2, UNITS, 4 * WIDE)
 
     vmem = pl.BlockSpec(memory_space=pltpu.VMEM)
     block = (ROWS, WIDE, LANES)
@@ -558,12 +564,16 @@
             jax.ShapeDtypeStruct(block, BF),
             jax.ShapeDtypeStruct((units, 4 * channels), F32),
             jax.ShapeDtypeStruct((units, 4 * channels), F32),
-            jax.ShapeDtypeStruct((152, LANES), F32),
-            jax.ShapeDtypeStruct((WIDE, LANES), F32),
+            jax.ShapeDtypeStruct((1, units), F32),
+            jax.ShapeDtypeStruct((3, 3, channels), F32),
         ],
-        in_specs=[vmem] * 7,
+        in_specs=[vmem] * 9,
         out_specs=[vmem] * 5,
         scratch_shapes=[
+            pltpu.VMEM((2, UNITS, 3 * LANES), F32),
+            pltpu.VMEM((2, UNITS, 4 * WIDE), BF),
+            pltpu.VMEM((8, 2 * LANES), F32),
+            pltpu.VMEM((3 * LANES, LANES), F32),
             pltpu.VMEM((3, ROWS + 4, WIDE, LANES), F32),
             pltpu.VMEM((3, ROWS + 4, WIDE, LANES), F32),
             pltpu.VMEM((9, WIDE, LANES), F32),
@@ -617,14 +627,16 @@
         swath_offset.reshape(1, -1),
         swath_value.reshape(1, -1),
         depth_kernel,
-        weights,
+        expand_weight.T,
+        project_weight,
+        expand_bias.reshape(1, -1),
     )
     return (
         jnp.transpose(state[:, :channels], (1, 0, 2)),
         expand.T,
         project,
-        bias_grad[:units, channels],
-        kernel_grad[:channels, :9].T.reshape(3, 3, channels),
+        bias_grad.reshape(-1),
+        kernel_grad,
     )
 
 

time: 99 us -> 97.9 us (0.989)
  Pallas kernels: 85.2 us -> 87.9 us
  local copies, waits for them, and re-layouts: 11.2 us -> 8.76 us
  other arithmetic: 0.99 us -> 0 us
    pallas_call x1, Pallas kernels: 85.2 us -> 87.9 us  [on_device(): pl.pallas_call(functools.partial(step_kernel, scale, n_lon, n_lat), out_s...]
    reshape x3 -> x0, local copies, waits for them, and re-layouts: 1.79 us -> none  [the longest x2 1.18 us: spread(): w = w.reshape(units, 4, channels)]
    unnamed x21 -> x17, local copies, waits for them, and re-layouts: 5.12 us -> 5.83 us
where the time goes in v6:
time: 97.9 us; the launch traced here: 97.3 us
  Pallas kernels  87.9 us (90%)
  local copies, waits for them, and re-layouts  8.76 us (9%)
    pallas_call x1, Pallas kernels, on_device(): pl.pallas_call(functools.partial(step_kernel, scale, n_lon, n_lat), out_s...  87.9 us
    unnamed x17, local copies, waits for them, and re-layouts  5.83 us

profile of v6, /device:TPU:24, one launch (start us, length us, event | category | flops | bytes accessed | tf_op | source)
XLA Modules:
  0.0 97.3 jit_solution(9586583350012597397)
XLA Ops:
  0.6 1.3 %copy.20 = bf16[75,32,128]{2,0,1:T(8,128)(2,1)S(1)} copy(bf16[75,32,128]{2,1,0:T(8,128)(2,1)} %param.9) | data formatting | bytes 1228800 | tf_op args[0]
  2.0 0.0 copy-start
  2.0 0.9 pad.7.state
  2.9 0.4 copy-done
  3.3 0.2 copy.19
  3.5 0.9 pad.8.grad
  4.4 87.9 %shard_map.128 = (bf16[32,80,128]{2,1,0:T(8,128)(2,1)}, f32[150,300]{1,0:T(8,128)}, f32[150,300]{1,0:T(8,128)}, f32[1,150]{1,0:T(1,128)}, f32[3,3,75]{2,1,0:T(4,128)}) custom-call(bf16[32,80,128]{2,1,0:T(8,128)(2,1)} %pad.7.state, bf16[32,80,128]{2,1,0:T(8,128)(2,1)} %pad.8.grad, s32[32,128]{1,0:T(8,128)} %land.1, s32[1,512]{1,0:T(1,128)} %bitcast.18, ...), custom_call_target="tpu_custom_call" | custom-call | tf_op jit(solution)/shard_map/pallas_call | solution.py:561
  92.3 1.1 %slice_bitcast_fusion = bf16[75,32,128]{2,0,1:T(8,128)(2,1)S(1)} fusion(bf16[32,80,128]{2,1,0:T(8,128)(2,1)} %get-tuple-element.10), kind=kLoop, calls=%fused_computation.2 | loop fusion | bytes 1228800 | tf_op jit(solution)/shard_map/transpose | solution.py:635
  93.4 0.0 copy-start.2
  93.4 1.0 %copy.16 = bf16[75,32,128]{2,1,0:T(8,128)(2,1)} copy(bf16[75,32,128]{2,0,1:T(8,128)(2,1)S(1)} %slice_bitcast_fusion) | data formatting | bytes 1228800
  94.4 0.0 copy-done.2
  94.4 0.0 copy-start.1
  94.4 0.7 copy.25
  95.1 0.3 copy-done.1
  95.5 0.0 copy-start.4
  95.5 0.0 copy-start.3
  95.5 0.7 copy.26
  96.2 0.0 copy-done.4
  96.2 0.6 copy.27
  96.7 0.0 copy-done.3
  96.7 0.6 copy.28
Async XLA Ops:
  2.0 1.3 %copy-start = (bf16[75,32,128]{2,1,0:T(8,128)(2,1)S(1)}, bf16[75,32,128]{2,1,0:T(8,128)(2,1)}, u32[]{:S(2)}) copy-start(bf16[75,32,128]{2,1,0:T(8,128)(2,1)} %param.11) | copy-start | bytes 1843204
  93.4 1.0 %copy-start.2 = (f32[150,300]{1,0:T(8,128)S(1)}, f32[150,300]{1,0:T(8,128)}, u32[]{:S(2)}) copy-start(f32[150,300]{1,0:T(8,128)} %get-tuple-element.11) | copy-start | bytes 540004
  94.4 1.0 %copy-start.1 = (f32[150,300]{1,0:T(8,128)S(1)}, f32[150,300]{1,0:T(8,128)}, u32[]{:S(2)}) copy-start(f32[150,300]{1,0:T(8,128)} %get-tuple-element.27) | copy-start | bytes 540004
  95.5 0.7 copy-start.4
  95.5 1.3 %copy-start.3 = (f32[3,3,75]{2,1,0:T(4,128)S(1)}, f32[3,3,75]{2,1,0:T(4,128)}, u32[]{:S(2)}) copy-start(f32[3,3,75]{2,1,0:T(4,128)} %get-tuple-element.29) | copy-start | bytes 8104

commit v7 on v6

--- a/solution.py
+++ b/solution.py
@@ -242,6 +242,8 @@
     rows_loop(0, ROWS, cotan_rows)
     for q in range(4):
         scatter(q, cotan.at[pl.ds(SHARE * q, SHARE)], cot_all.at[ch], cs.at[q], cr.at[ch])
+    wait_edges(0)
+    send_rows(0, fwin)
     units, channels = project.shape[0], project.shape[1] // 4
     spread_out[...] = jnp.zeros_like(spread_out)
     bias_row[...] = jnp.zeros_like(bias_row)
@@ -267,11 +269,7 @@
         column = jnp.where(diagonal, tap_rows[t : t + 1, :], 0.0)
         kb[t] = jnp.broadcast_to(jnp.sum(column, axis=1, keepdims=True), (WIDE, LANES))
 
-    wait_edges(0)
-    send_rows(0, fwin)
     inner_windows(0, fwin)
-    to_across.wait()
-    passed.start()
 
     def conv_piece(c):
         for g in range(WIDE // 16):
@@ -301,6 +299,8 @@
     for c in (3, 0):
         conv_piece(c)
         send_conv(c)
+    to_across.wait()
+    passed.start()
 
     to_mate.wait()
     acc_p[...] = jnp.zeros_like(acc_p)

time: 97.9 us -> 101 us (1.032)
  Pallas kernels: 87.9 us -> 90.6 us
    pallas_call x1, Pallas kernels: 87.9 us -> 90.6 us  [on_device(): pl.pallas_call(functools.partial(step_kernel, scale, n_lon, n_lat), out_s...]
where the time goes in v7:
time: 101 us; the launch traced here: 100 us
  Pallas kernels  90.6 us (90%)
  local copies, waits for them, and re-layouts  8.76 us (9%)
    pallas_call x1, Pallas kernels, on_device(): pl.pallas_call(functools.partial(step_kernel, scale, n_lon, n_lat), out_s...  90.6 us
    unnamed x17, local copies, waits for them, and re-layouts  5.83 us

profile of v7, /device:TPU:24, one launch (start us, length us, event | category | flops | bytes accessed | tf_op | source)
XLA Modules:
  0.0 100.0 jit_solution(17688744982867602835)
XLA Ops:
  0.6 1.3 %copy.20 = bf16[75,32,128]{2,0,1:T(8,128)(2,1)S(1)} copy(bf16[75,32,128]{2,1,0:T(8,128)(2,1)} %param.9) | data formatting | bytes 1228800 | tf_op args[0]
  2.0 0.0 copy-start
  2.0 0.9 pad.7.state
  2.9 0.4 copy-done
  3.3 0.2 copy.19
  3.5 0.9 pad.8.grad
  4.4 90.6 %shard_map.128 = (bf16[32,80,128]{2,1,0:T(8,128)(2,1)}, f32[150,300]{1,0:T(8,128)}, f32[150,300]{1,0:T(8,128)}, f32[1,150]{1,0:T(1,128)}, f32[3,3,75]{2,1,0:T(4,128)}) custom-call(bf16[32,80,128]{2,1,0:T(8,128)(2,1)} %pad.7.state, bf16[32,80,128]{2,1,0:T(8,128)(2,1)} %pad.8.grad, s32[32,128]{1,0:T(8,128)} %land.1, s32[1,512]{1,0:T(1,128)} %bitcast.18, ...), custom_call_target="tpu_custom_call" | custom-call | tf_op jit(solution)/shard_map/pallas_call | solution.py:561
  95.0 1.1 %slice_bitcast_fusion = bf16[75,32,128]{2,0,1:T(8,128)(2,1)S(1)} fusion(bf16[32,80,128]{2,1,0:T(8,128)(2,1)} %get-tuple-element.10), kind=kLoop, calls=%fused_computation.2 | loop fusion | bytes 1228800 | tf_op jit(solution)/shard_map/transpose | solution.py:635
  96.1 0.0 copy-start.2
  96.1 1.0 copy.16
  97.1 0.0 copy-done.2
  97.1 0.0 copy-start.1
  97.1 0.7 copy.25
  97.8 0.3 copy-done.1
  98.1 0.0 copy-start.4
  98.1 0.0 copy-start.3
  98.2 0.7 copy.26
  98.8 0.0 copy-done.4
  98.8 0.6 copy.27
  99.4 0.0 copy-done.3
  99.4 0.6 copy.28
Async XLA Ops:
  2.0 1.3 %copy-start = (bf16[75,32,128]{2,1,0:T(8,128)(2,1)S(1)}, bf16[75,32,128]{2,1,0:T(8,128)(2,1)}, u32[]{:S(2)}) copy-start(bf16[75,32,128]{2,1,0:T(8,128)(2,1)} %param.11) | copy-start | bytes 1843204
  96.1 1.0 copy-start.2
  97.1 1.0 %copy-start.1 = (f32[150,300]{1,0:T(8,128)S(1)}, f32[150,300]{1,0:T(8,128)}, u32[]{:S(2)}) copy-start(f32[150,300]{1,0:T(8,128)} %get-tuple-element.27) | copy-start | bytes 540004
  98.1 0.7 copy-start.4
  98.1 1.3 %copy-start.3 = (f32[3,3,75]{2,1,0:T(4,128)S(1)}, f32[3,3,75]{2,1,0:T(4,128)}, u32[]{:S(2)}) copy-start(f32[3,3,75]{2,1,0:T(4,128)} %get-tuple-element.29) | copy-start | bytes 8104
